TPU v7x, 512 devices: a whole 4x4x16 slice. The times are simulated.
512 devices in a mesh: dp: 64 (over z_hi, x, y), tensor: 8 (over z_lo, core).
Axes of the slice: x: 4, y: 4, z: 16 (z_hi: 4, z_lo: 4; z = z_hi * 4 + z_lo), core: 2. Of those that a mesh axis runs over, the one named last changes fastest.
Arguments:
- queries: bfloat16 [32768, 3072], P('dp', 'tensor'), may hold values from -6 to 6
- key_rows: bfloat16 [32768, 3072], P('dp', 'tensor'), may hold values from -6 to 6
- value_rows: bfloat16 [32768, 3072], P('dp', 'tensor'), may hold values from -6 to 6
- out_weight: bfloat16 [2560, 3072], P(None, 'tensor'), may hold values from -0.109375 to 0.109375
- grad_out: bfloat16 [32768, 2560], P(('dp', 'tensor')), may hold values from -48 to 48
Outputs:
- grad_query: bfloat16 [32768, 3072], P('dp', 'tensor')
- grad_keys: bfloat16 [32768, 3072], P('dp', 'tensor')
- grad_values: bfloat16 [32768, 3072], P('dp', 'tensor')
- grad_weight: float32 [2560, 3072], P('dp', 'tensor')
All inputs are finite; a program needn't handle non-finite values.
Results may differ from a plain program's by a relative error of at most 0.013.
Values may be sent and summed in bfloat16 or wider, within the bound.
No kernel may reach another device: no remote copies, remote signals or barrier semaphores. Data moves between devices by JAX's collectives and lax.ppermute only.
A program may use at most 64 MiB of HBM per device.

v0:
```python
import math

import jax
import jax.numpy as jnp
from jax import lax
from jax.sharding import PartitionSpec as P

HEAD = 128
LENGTH = 256


def attention_probs(query_heads, key_heads):
    scaling = 1.0 / math.sqrt(HEAD)
    scores = (
        jnp.einsum("sqhe,skhe->shqk", query_heads, key_heads, preferred_element_type=jnp.float32)
        * scaling
    )
    length = query_heads.shape[1]
    causal = lax.broadcasted_iota(jnp.int32, (length, length), 0) >= lax.broadcasted_iota(
        jnp.int32, (length, length), 1
    )
    scores = jnp.where(causal[None, None, :, :], scores, -jnp.inf)
    row_max = jnp.max(scores, axis=-1, keepdims=True)
    exp_scores = jnp.exp(scores - row_max)
    return exp_scores / jnp.sum(exp_scores, axis=-1, keepdims=True)


def on_device(queries, key_rows, value_rows, out_weight, grad_out):
    tokens_here = queries.shape[0]
    head_width = queries.shape[1]
    heads_here = head_width // HEAD
    seqs_here = tokens_here // LENGTH
    scaling = 1.0 / math.sqrt(HEAD)
    head_shape = (seqs_here, LENGTH, heads_here, HEAD)
    query_heads = queries.reshape(head_shape)
    key_heads = key_rows.reshape(head_shape)
    value_heads = value_rows.reshape(head_shape)
    probs = attention_probs(query_heads, key_heads)
    probs_low = probs.astype(jnp.bfloat16)
    attended = jnp.einsum(
        "shqk,skhe->sqhe", probs_low, value_heads, preferred_element_type=jnp.float32
    )
    attended = attended.astype(jnp.bfloat16).reshape(tokens_here, head_width)
    block_rows = lax.all_gather(grad_out, "tensor", axis=0, tiled=True)
    grad_part = jnp.dot(block_rows, out_weight, preferred_element_type=jnp.float32).astype(
        jnp.bfloat16
    )
    grad_attended = grad_part
    weight_grad = lax.dot_general(
        block_rows, attended, (((0,), (0,)), ((), ())), preferred_element_type=jnp.float32
    )
    grad_attended, carried = (grad_attended, weight_grad)
    my_share = lax.psum_scatter(carried, "dp", scatter_dimension=0, tiled=True)
    grad_weight = my_share * (1.0 / lax.axis_size("dp"))
    grad_heads = grad_attended.reshape(head_shape)
    grad_values = jnp.einsum(
        "shqk,sqhe->skhe", probs_low, grad_heads, preferred_element_type=jnp.float32
    ).astype(jnp.bfloat16)
    grad_probs = jnp.einsum(
        "sqhe,skhe->shqk", grad_heads, value_heads, preferred_element_type=jnp.float32
    )
    row_total = jnp.sum(probs * grad_probs, axis=-1, keepdims=True)
    grad_scores = (probs * (grad_probs - row_total) * scaling).astype(jnp.bfloat16)
    grad_query = jnp.einsum(
        "shqk,skhe->sqhe", grad_scores, key_heads, preferred_element_type=jnp.float32
    ).astype(jnp.bfloat16)
    grad_keys = jnp.einsum(
        "shqk,sqhe->skhe", grad_scores, query_heads, preferred_element_type=jnp.float32
    ).astype(jnp.bfloat16)
    return (
        grad_query.reshape(tokens_here, head_width),
        grad_keys.reshape(tokens_here, head_width),
        grad_values.reshape(tokens_here, head_width),
        grad_weight,
    )


def solution(mesh):
    return jax.shard_map(
        on_device,
        mesh=mesh,
        in_specs=(
            P("dp", "tensor"),
            P("dp", "tensor"),
            P("dp", "tensor"),
            P(None, "tensor"),
            P(("dp", "tensor"), None),
        ),
        out_specs=(P("dp", "tensor"), P("dp", "tensor"), P("dp", "tensor"), P("dp", "tensor")),
        check_vma=False,
    )
```

profile of v0, /device:TPU:16, one launch (start us, length us, event | category | flops | bytes accessed | tf_op | source)
XLA Modules:
  0.0 944.9 jit_solution(15900221146341785928)
XLA Ops:
  7.2 0.0 copy-start
  7.2 0.0 all-gather.2.cloned.1.call-start
  7.2 0.7 all-gather.2.cloned.1.call-update
  7.9 0.0 all-reduce.3.cloned.1.call-start
  8.0 1.4 reshape.56
  9.4 0.0 copy-start.3
  9.4 1.6 reshape.57
  11.0 0.0 copy-start.1
  11.0 1.6 reshape.58
  12.6 0.7 iota_compare_fusion
  13.2 2.6 fusion.53
  15.8 0.0 copy-done.3
  15.8 0.0 copy-done.1
  15.8 1.8 fusion.26
  17.7 0.6 copy.62
  18.3 0.1 copy.89
  18.3 42.0 %all-gather.2.cloned.1.call-done = bf16[512,2560]{1,0:T(8,128)(2,1)} async-done(((bf16[64,2560]{1,0:T(8,128)(2,1)}), bf16[512,2560]{1,0:T(8,128)(2,1)}) %all-gather.2.cloned.1.call-update) | async-done | bytes 2621456 | tf_op jit(solution)/shard_map/all_gather | solution.py:44
  60.3 4.8 convolution_bitcast_fusion
  65.1 0.0 all-reduce.3.cloned.1.call-update
  65.2 1.3 dynamic-slice
  67.1 0.0 copy-done
  67.1 3.3 convolution_convert_fusion.2
  70.4 0.1 reshape.59
  70.5 0.2 copy.57
  70.7 0.0 copy-start.4
  70.7 1.6 fusion.32
  72.3 0.0 copy-done.4
  72.3 4.2 fusion.19
  76.6 1.3 copy.71
  77.9 0.0 copy-start.2
  77.9 2.6 fusion.25
  80.5 1.3 copy.72
  81.8 0.0 copy-done.2
  81.8 4.4 fusion.22
  86.2 1.3 copy.70
  87.6 0.8 copy.117
  88.4 1.0 copy_bitcast_fusion
  89.4 846.9 %all-reduce.3.cloned.1.call-done = f32[2560,384]{0,1:T(8,128)} async-done(((f32[2560,384]{0,1:T(8,128)}), f32[2560,384]{0,1:T(8,128)}) %all-reduce.3.cloned.1.call-update) | async-done | bytes 3932176
  936.2 1.1 dynamic-slice_multiply_fusion
  937.4 0.7 copy.66
Async XLA Ops:
  7.2 59.9 %copy-start = (bf16[2560,384]{1,0:T(8,128)(2,1)S(1)}, bf16[2560,384]{1,0:T(8,128)(2,1)}, u32[]{:S(2)}) copy-start(bf16[2560,384]{1,0:T(8,128)(2,1)} %param.8) | copy-start | bytes 5898244
  7.2 53.1 %all-gather.2.cloned.1.call-start = ((), (), s32[]{:S(2)}) async-start(), calls=%async_computation | async-start | bytes 2949120 | tf_op jit(solution)/shard_map/all_gather | solution.py:44
  7.9 928.3 %all-reduce.3.cloned.1.call-start = ((), (), s32[]{:S(2)}) async-start(), calls=%async_computation.1 | async-start | bytes 7864320
  9.4 6.5 copy-start.3
  11.0 4.9 copy-start.1
  70.7 1.6 copy-start.4
  77.9 3.9 copy-start.2
Sparse Core Ops, SparseCore 0:
  10.1 50.1 all-gather.1
  65.3 870.9 all-reduce.2
where the time goes:
time: 945 us
  waiting for transfers between devices  890 us (94%)
  matrix products  25.4 us (3%)
  between operations  14.8 us (2%)
  local copies, waits for them, and re-layouts  13.3 us (1%)
    unnamed x3, waiting for transfers between devices  848 us
    all_gather x1, waiting for transfers between devices, on_device(): block_rows = lax.all_gather(grad_out, 'tensor', axis=0, tiled=True)  42 us
  transfers between devices with their start and end apart: 2, of which 2 were waited for; matrix products, arithmetic and copies ran while one was open for 4% of the time, Pallas kernels for 0%

commit v1 on v0

v1 whole, which is shorter than its diff:
```python
import math

import jax
import jax.numpy as jnp
import numpy as np
from jax import lax
from jax.experimental import pallas as pl
from jax.experimental.pallas import tpu as pltpu
from jax.sharding import Mesh, PartitionSpec as P

HEAD = 128
LENGTH = 256
SCALING = 1.0 / math.sqrt(HEAD)
F32 = jnp.float32
BF16 = jnp.bfloat16
AXES = ("zh", "x", "y", "zl", "core")


def dot(a, b, ca, cb):
    return lax.dot_general(a, b, (((ca,), (cb,)), ((), ())), preferred_element_type=F32)


def head_probs(q, k):
    scores = dot(q, k, 1, 1) * SCALING
    n = scores.shape[0]
    causal = lax.broadcasted_iota(jnp.int32, (n, n), 0) >= lax.broadcasted_iota(
        jnp.int32, (n, n), 1
    )
    scores = jnp.where(causal, scores, -jnp.inf)
    row_max = jnp.max(scores, axis=1, keepdims=True)
    exp_scores = jnp.exp(scores - row_max)
    return exp_scores * (1.0 / jnp.sum(exp_scores, axis=1, keepdims=True))


def tiles(shape):
    for s in range(shape[0] // LENGTH):
        for h in range(shape[1] // HEAD):
            yield pl.ds(s * LENGTH, LENGTH), pl.ds(h * HEAD, HEAD)


def attended_kernel(q_ref, k_ref, v_ref, out_ref):
    for at in tiles(out_ref.shape):
        probs = head_probs(q_ref[at], k_ref[at])
        out_ref[at] = dot(probs.astype(BF16), v_ref[at], 1, 0).astype(BF16)


def weight_kernel(rows_ref, attended_ref, out_ref):
    part = dot(rows_ref[...], attended_ref[...], 0, 0)
    out_ref[...] = part.astype(BF16).reshape(out_ref.shape)


def backward_kernel(q_ref, k_ref, v_ref, rows_ref, w_ref, gq_ref, gk_ref, gv_ref, g_ref):
    g_ref[...] = dot(rows_ref[...], w_ref[...], 1, 0).astype(BF16)
    for at in tiles(gq_ref.shape):
        q, k, v, g = q_ref[at], k_ref[at], v_ref[at], g_ref[at]
        probs = head_probs(q, k)
        gv_ref[at] = dot(probs.astype(BF16), g, 0, 0).astype(BF16)
        grad_probs = dot(g, v, 1, 1)
        row_total = jnp.sum(probs * grad_probs, axis=1, keepdims=True)
        grad_scores = (probs * (grad_probs - row_total) * SCALING).astype(BF16)
        gq_ref[at] = dot(grad_scores, k, 1, 0).astype(BF16)
        gk_ref[at] = dot(grad_scores, q, 0, 0).astype(BF16)


def call(kernel, outs, *args, scratch=()):
    return pl.pallas_call(
        kernel,
        out_shape=outs,
        scratch_shapes=scratch,
        compiler_params=pltpu.CompilerParams(vmem_limit_bytes=48 * 2**20),
        name=kernel.__name__,
    )(*args)


def gather_rows(mine):
    zl, core = lax.axis_index("zl"), lax.axis_index("core")
    far = lax.ppermute(mine, "zl", [(0, 2), (2, 0), (1, 3), (3, 1)])
    inner = lax.ppermute(mine, "zl", [(1, 2), (2, 1)])
    near = lax.ppermute(mine, "zl", [(0, 1), (1, 0), (2, 3), (3, 2)])
    outer = lax.ppermute(far, "zl", [(1, 0), (2, 3)])
    last = jnp.where((zl == 1) | (zl == 2), inner, outer)
    pieces = jnp.stack([mine, near, far, last])
    pieces = jnp.take(pieces, jnp.arange(4) ^ zl, axis=0)
    other = lax.ppermute(pieces, "core", [(0, 1), (1, 0)])
    first = jnp.where(core == 0, pieces, other)
    second = jnp.where(core == 0, other, pieces)
    return jnp.stack([first, second], axis=1).reshape(8 * mine.shape[0], mine.shape[1])


def on_device(queries, key_rows, value_rows, out_weight, grad_out):
    shape = queries.shape
    same = jax.ShapeDtypeStruct(shape, BF16)
    attended = call(attended_kernel, same, queries, key_rows, value_rows)
    rows = gather_rows(grad_out)
    d = out_weight.shape[0]
    n_dp = 64
    part = call(
        weight_kernel, jax.ShapeDtypeStruct((4, 16, d // n_dp, shape[1]), BF16), rows, attended
    )
    part = part.transpose(1, 0, 2, 3)
    got = lax.all_to_all(part, ("x", "y"), 0, 0, tiled=True)
    plane = jnp.sum(got.astype(F32), axis=0).astype(BF16)
    zh = lax.axis_index("zh")
    total = lax.dynamic_index_in_dim(plane, zh, 0, keepdims=False).astype(F32)
    for step in (2, 1, 3):
        piece = lax.dynamic_index_in_dim(plane, (zh + step) % 4, 0, keepdims=False)
        total += lax.ppermute(piece, "zh", [(i, (i + step) % 4) for i in range(4)]).astype(F32)
    grad_weight = total * (1.0 / n_dp)
    gq, gk, gv = call(
        backward_kernel,
        (same, same, same),
        queries,
        key_rows,
        value_rows,
        rows,
        out_weight,
        scratch=[pltpu.VMEM(shape, BF16)],
    )
    return gq, gk, gv, grad_weight


def solution(mesh):
    split = Mesh(np.asarray(mesh.devices).reshape(4, 4, 4, 4, 2), AXES)
    dp, tensor = ("zh", "x", "y"), ("zl", "core")
    return jax.shard_map(
        on_device,
        mesh=split,
        in_specs=(P(dp, tensor), P(dp, tensor), P(dp, tensor), P(None, tensor), P(AXES, None)),
        out_specs=(P(dp, tensor), P(dp, tensor), P(dp, tensor), P(dp, tensor)),
        check_vma=False,
    )
```

time: 945 us -> 118 us (0.12)
  the two profiles are of different devices: /device:TPU:16 before, /device:TPU:8 now
where the time goes in v1:
time: 118 us
  waiting for transfers between devices  48.9 us (41%)
  starting transfers between devices  46.4 us (39%)
  Pallas kernels  8.65 us (7%)
  other arithmetic  7.53 us (6%)
  local copies, waits for them, and re-layouts  5.45 us (5%)
    all_to_all x1, waiting for transfers between devices, on_device(): got = lax.all_to_all(part, ('x', 'y'), 0, 0, tiled=True)  28 us
    ppermute x3, starting transfers between devices, on_device(): lax.ppermute(piece, 'zh', [(i, (i + step) % 4) for i in range(4)])  24.9 us
    ppermute x1, waiting for transfers between devices, gather_rows(): far = lax.ppermute(mine, 'zl', [(0, 2), (2, 0), (1, 3), (3, 1)])  10 us
    ppermute x1, waiting for transfers between devices, gather_rows(): outer = lax.ppermute(far, 'zl', [(1, 0), (2, 3)])  8.84 us
    pallas_call x3, Pallas kernels, call(): pl.pallas_call(kernel, out_shape=outs, scratch_shapes=scratch, compiler_p...  8.65 us
    all_to_all x1, starting transfers between devices, on_device(): got = lax.all_to_all(part, ('x', 'y'), 0, 0, tiled=True)  7.39 us
    ppermute x1, starting transfers between devices, gather_rows(): far = lax.ppermute(mine, 'zl', [(0, 2), (2, 0), (1, 3), (3, 1)])  5.18 us
    ppermute x1, starting transfers between devices, gather_rows(): near = lax.ppermute(mine, 'zl', [(0, 1), (1, 0), (2, 3), (3, 2)])  5.07 us
  transfers between devices with their start and end apart: 9, of which 4 were waited for; matrix products, arithmetic and copies ran while one was open for 0% of the time, Pallas kernels for 6%

profile of v1, /device:TPU:8, one launch (start us, length us, event | category | flops | bytes accessed | tf_op | source)
XLA Modules:
  0.0 117.8 jit_solution(16666970632213446912)
XLA Ops:
  0.6 5.2 %collective-permute-start.1 = (bf16[64,2560]{1,0:T(8,128)(2,1)}, bf16[64,2560]{1,0:T(8,128)(2,1)S(1)}, u32[]{:S(2)}, u32[]{:S(2)}) collective-permute-start(bf16[64,2560]{1,0:T(8,128)(2,1)} %param.9), channel_id=1, source_target_pairs={{0,4},{4,0},{2,6},{6,2},{1,5},{5,1},{3,7},{7,3},{8,12},{12,8},{10,... | collective-permute-start | bytes 983048 | tf_op jit(solution)/shard_map/ppermute | solution.py:77
  5.8 0.7 collective-permute-start.2
  6.5 5.1 %collective-permute-start = (bf16[64,2560]{1,0:T(8,128)(2,1)}, bf16[64,2560]{1,0:T(8,128)(2,1)S(1)}, u32[]{:S(2)}, u32[]{:S(2)}) collective-permute-start(bf16[64,2560]{1,0:T(8,128)(2,1)} %param.9), channel_id=1, source_target_pairs={{0,2},{2,0},{4,6},{6,4},{1,3},{3,1},{5,7},{7,5},{8,10},{10,8},{12,... | collective-permute-start | bytes 983048 | tf_op jit(solution)/shard_map/ppermute | solution.py:79
  11.6 10.0 %collective-permute-done.1 = bf16[64,2560]{1,0:T(8,128)(2,1)S(1)} collective-permute-done((bf16[64,2560]{1,0:T(8,128)(2,1)}, bf16[64,2560]{1,0:T(8,128)(2,1)S(1)}, u32[]{:S(2)}, u32[]{:S(2)}) %collective-permute-start.1) | collective-permute-done | bytes 327712 | tf_op jit(solution)/shard_map/ppermute | solution.py:77
  21.6 1.3 %collective-permute-start.3 = (bf16[64,2560]{1,0:T(8,128)(2,1)S(1)}, bf16[64,2560]{1,0:T(8,128)(2,1)S(1)}, u32[]{:S(2)}, u32[]{:S(2)}) collective-permute-start(bf16[64,2560]{1,0:T(8,128)(2,1)S(1)} %collective-permute-done.1), channel_id=1, source_target_pairs={{2,0},{4,6},{3,1},{5,7},{10,8},{12,14},{11,9},{13,15},{18,16},{20,... | collective-permute-start | bytes 983048 | tf_op jit(solution)/shard_map/ppermute | solution.py:80
  22.9 0.0 collective-permute-done.2
  23.0 8.8 %collective-permute-done.3 = bf16[64,2560]{1,0:T(8,128)(2,1)S(1)} collective-permute-done((bf16[64,2560]{1,0:T(8,128)(2,1)S(1)}, bf16[64,2560]{1,0:T(8,128)(2,1)S(1)}, u32[]{:S(2)}, u32[]{:S(2)}) %collective-permute-start.3) | collective-permute-done | bytes 327712 | tf_op jit(solution)/shard_map/ppermute | solution.py:80
  31.8 0.0 collective-permute-done
  31.9 1.1 pad_maximum_fusion.1
  33.0 0.6 gather_fusion
  33.6 0.0 copy-start.1
  33.6 0.0 copy-start.2
  33.7 0.0 copy-start.3
  33.7 1.3 %broadcast_select_fusion = bf16[4,64,2560]{2,1,0:T(8,128)(2,1)} fusion(bf16[4,64,2560]{2,1,0:T(8,128)(2,1)S(1)} %gather_fusion, pred[4]{0:T(512)(128)(4,1)S(1)} %compare_and_fusion), kind=kLoop, calls=%fused_computation.5 | loop fusion | flops 655360 | bytes 2621444 | tf_op jit(solution)/shard_map/jit(_take)/select_n | solution.py:83
  34.9 1.9 %collective-permute-start.4 = (bf16[4,64,2560]{2,1,0:T(8,128)(2,1)}, bf16[4,64,2560]{2,1,0:T(8,128)(2,1)}, u32[]{:S(2)}, u32[]{:S(2)}) collective-permute-start(bf16[4,64,2560]{2,1,0:T(8,128)(2,1)} %broadcast_select_fusion), channel_id=1, source_target_pairs={{0,1},{1,0},{2,3},{3,2},{4,5},{5,4},{6,7},{7,6},{8,9},{9,8},{10,11... | collective-permute-start | bytes 3932168 | tf_op jit(solution)/shard_map/ppermute | solution.py:84
  36.9 0.0 copy-done.1
  36.9 0.0 copy-done.2
  36.9 0.0 copy-done.3
  36.9 1.3 %attended_kernel.1.attended_ref = bf16[512,384]{1,0:T(8,128)(2,1)S(1)} custom-call(bf16[512,384]{1,0:T(8,128)(2,1)S(1)} %copy-done.1, bf16[512,384]{1,0:T(8,128)(2,1)S(1)} %copy-done.2, bf16[512,384]{1,0:T(8,128)(2,1)S(1)} %copy-done.3), custom_call_target="tpu_custom_call" | custom-call | tf_op jit(solution)/shard_map/attended_kernel/pallas_call | solution.py:66
  38.2 2.0 %collective-permute-done.4 = bf16[4,64,2560]{2,1,0:T(8,128)(2,1)} collective-permute-done((bf16[4,64,2560]{2,1,0:T(8,128)(2,1)}, bf16[4,64,2560]{2,1,0:T(8,128)(2,1)}, u32[]{:S(2)}, u32[]{:S(2)}) %collective-permute-start.4) | collective-permute-done | bytes 1310752 | tf_op jit(solution)/shard_map/ppermute | solution.py:84
  40.2 1.6 %select_bitcast_fusion.1 = (bf16[4,1,64,2560]{3,2,0,1:T(8,128)(2,1)S(1)}, bf16[4,1,64,2560]{3,2,0,1:T(8,128)(2,1)S(1)}) fusion(bf16[4,64,2560]{2,1,0:T(8,128)(2,1)} %collective-permute-done.4, pred[]{:T(512)S(6)} %eq.14, bf16[4,64,2560]{2,1,0:T(8,128)(2,1)S(1)} %gather_fusion, pred[4]{0:T(512)(128)(4,1)S(1)} %compare_and_fusion), kind=kLoop, calls=%fused_computation.4 | loop fusion | flops 1966080 | bytes 5242885 | tf_op jit(solution)/shard_map/stack | solution.py:87
  41.8 0.2 pad_maximum_fusion
  42.0 0.2 copy.10
  42.2 1.6 %weight_kernel.1 = bf16[4,16,40,384]{3,2,1,0:T(8,128)(2,1)S(1)} custom-call(bf16[512,2560]{1,0:T(8,128)(2,1)S(1)} %bitcast.22, bf16[512,384]{1,0:T(8,128)(2,1)S(1)} %attended_kernel.1.attended_ref), custom_call_target="tpu_custom_call" | custom-call | tf_op jit(solution)/shard_map/weight_kernel/pallas_call | solution.py:66
  43.7 1.5 %copy.11 = bf16[16,4,40,384]{3,2,1,0:T(8,128)(2,1)} copy(bf16[16,4,40,384]{3,2,0,1:T(8,128)(2,1)S(1)} %bitcast.24) | data formatting | bytes 3932160 | tf_op jit(solution)/shard_map/transpose | solution.py:100
  45.2 7.4 %all-to-all-start = ((bf16[16,4,40,384]{3,2,1,0:T(8,128)(2,1)}), bf16[16,4,40,384]{3,2,1,0:T(8,128)(2,1)}, u32[]{:S(2)}, u32[]{:S(2)}) async-start(bf16[16,4,40,384]{3,2,1,0:T(8,128)(2,1)} %copy.11), calls=%async_computation | async-start | bytes 3932160 | tf_op jit(solution)/shard_map/all_to_all | solution.py:101
  52.6 28.0 %all-to-all-done = bf16[16,4,40,384]{3,2,1,0:T(8,128)(2,1)} async-done(((bf16[16,4,40,384]{3,2,1,0:T(8,128)(2,1)}), bf16[16,4,40,384]{3,2,1,0:T(8,128)(2,1)}, u32[]{:S(2)}, u32[]{:S(2)}) %all-to-all-start) | async-done | bytes 1966112 | tf_op jit(solution)/shard_map/all_to_all | solution.py:101
  80.6 1.8 %reduce_sum.12 = bf16[4,40,384]{2,1,0:T(8,128)(2,1)S(1)} reduce(bf16[16,4,40,384]{3,2,1,0:T(8,128)(2,1)} %all-to-all-done, bf16[]{:T(256)} %constant.64.clone.1), dimensions={0}, to_apply=%region_0.1 | reduce | flops 921600 | bytes 2088962 | tf_op jit(solution)/shard_map/reduce_sum | solution.py:102
  82.5 0.6 dynamic-slice_bitcast_fusion.2
  83.1 12.1 %collective-permute-start.7 = (bf16[40,384]{1,0:T(8,128)(2,1)}, bf16[40,384]{1,0:T(8,128)(2,1)}, u32[]{:S(2)}, u32[]{:S(2)}) collective-permute-start(bf16[40,384]{1,0:T(8,128)(2,1)} %get-tuple-element.13), channel_id=1, source_target_pairs={{0,384},{128,0},{256,128},{384,256},{1,385},{129,1},{257,129},{385... | collective-permute-start | bytes 92168 | tf_op jit(solution)/shard_map/ppermute | solution.py:107
  95.2 1.9 %collective-permute-start.6 = (bf16[40,384]{1,0:T(8,128)(2,1)}, bf16[40,384]{1,0:T(8,128)(2,1)}, u32[]{:S(2)}, u32[]{:S(2)}) collective-permute-start(bf16[40,384]{1,0:T(8,128)(2,1)} %get-tuple-element.14), channel_id=1, source_target_pairs={{0,128},{128,256},{256,384},{384,0},{1,129},{129,257},{257,385},{3... | collective-permute-start | bytes 92168 | tf_op jit(solution)/shard_map/ppermute | solution.py:107
  97.2 10.8 %collective-permute-start.5 = (bf16[40,384]{1,0:T(8,128)(2,1)}, bf16[40,384]{1,0:T(8,128)(2,1)}, u32[]{:S(2)}, u32[]{:S(2)}) collective-permute-start(bf16[40,384]{1,0:T(8,128)(2,1)} %get-tuple-element.12), channel_id=1, source_target_pairs={{0,256},{128,384},{256,0},{384,128},{1,257},{129,385},{257,1},{385... | collective-permute-start | bytes 92168 | tf_op jit(solution)/shard_map/ppermute | solution.py:107
  108.0 0.0 copy-start
  108.0 1.5 %copy-done = bf16[2560,384]{1,0:T(8,128)(2,1)S(1)} copy-done((bf16[2560,384]{1,0:T(8,128)(2,1)S(1)}, bf16[2560,384]{1,0:T(8,128)(2,1)}, u32[]{:S(2)}) %copy-start) | copy-done | bytes 1966104
  109.6 0.0 copy-start.4
  109.6 1.0 copy-done.4
  110.6 5.8 %backward_kernel.1 = (bf16[512,384]{1,0:T(8,128)(2,1)}, bf16[512,384]{1,0:T(8,128)(2,1)}, bf16[512,384]{1,0:T(8,128)(2,1)}) custom-call(bf16[512,384]{1,0:T(8,128)(2,1)S(1)} %copy-done.1, bf16[512,384]{1,0:T(8,128)(2,1)S(1)} %copy-done.2, bf16[512,384]{1,0:T(8,128)(2,1)S(1)} %copy-done.4, bf16[512,2560]{1,0:T(8,128)(2,1)S(1)} %bitcast.23, ...), custom_call_target="tpu_custom_call" | custom-call | tf_op jit(solution)/shard_map/backward_kernel/pallas_call | solution.py:66
  116.3 0.0 collective-permute-done.7
  116.3 0.0 collective-permute-done.6
  116.3 0.0 collective-permute-done.5
  116.3 1.4 %fusion.2 = f32[40,384]{1,0:T(8,128)} fusion(bf16[40,384]{1,0:T(8,128)(2,1)} %collective-permute-done.7, bf16[40,384]{1,0:T(8,128)(2,1)} %collective-permute-done.6, bf16[40,384]{1,0:T(8,128)(2,1)} %collective-permute-done.5, bf16[4,40,384]{2,1,0:T(8,128)(2,1)S(1)} %reduce_sum.12, s32[]{:T(128)S(6)} %select_n.76), kind=kLoop, calls=%fused_computation.10 | loop fusion | flops 122880 | bytes 184324 | tf_op jit(solution)/shard_map/mul | solution.py:108
  (4 shorter events, 0.1 us)
Async XLA Ops:
  0.6 21.0 %collective-permute-start.1 = (bf16[64,2560]{1,0:T(8,128)(2,1)}, bf16[64,2560]{1,0:T(8,128)(2,1)S(1)}, u32[]{:S(2)}, u32[]{:S(2)}) collective-permute-start(bf16[64,2560]{1,0:T(8,128)(2,1)} %param.9), channel_id=1, source_target_pairs={{0,4},{4,0},{2,6},{6,2},{1,5},{5,1},{3,7},{7,3},{8,12},{12,8},{10,... | collective-permute-start | bytes 983048 | tf_op jit(solution)/shard_map/ppermute | solution.py:77
  5.8 17.1 %collective-permute-start.2 = (bf16[64,2560]{1,0:T(8,128)(2,1)}, bf16[64,2560]{1,0:T(8,128)(2,1)S(1)}, u32[]{:S(2)}, u32[]{:S(2)}) collective-permute-start(bf16[64,2560]{1,0:T(8,128)(2,1)} %param.9), channel_id=1, source_target_pairs={{2,4},{4,2},{3,5},{5,3},{10,12},{12,10},{11,13},{13,11},{18,20},{2... | collective-permute-start | bytes 983048 | tf_op jit(solution)/shard_map/ppermute | solution.py:78
  6.5 25.3 %collective-permute-start = (bf16[64,2560]{1,0:T(8,128)(2,1)}, bf16[64,2560]{1,0:T(8,128)(2,1)S(1)}, u32[]{:S(2)}, u32[]{:S(2)}) collective-permute-start(bf16[64,2560]{1,0:T(8,128)(2,1)} %param.9), channel_id=1, source_target_pairs={{0,2},{2,0},{4,6},{6,4},{1,3},{3,1},{5,7},{7,5},{8,10},{10,8},{12,... | collective-permute-start | bytes 983048 | tf_op jit(solution)/shard_map/ppermute | solution.py:79
  21.6 10.2 %collective-permute-start.3 = (bf16[64,2560]{1,0:T(8,128)(2,1)S(1)}, bf16[64,2560]{1,0:T(8,128)(2,1)S(1)}, u32[]{:S(2)}, u32[]{:S(2)}) collective-permute-start(bf16[64,2560]{1,0:T(8,128)(2,1)S(1)} %collective-permute-done.1), channel_id=1, source_target_pairs={{2,0},{4,6},{3,1},{5,7},{10,8},{12,14},{11,9},{13,15},{18,16},{20,... | collective-permute-start | bytes 983048 | tf_op jit(solution)/shard_map/ppermute | solution.py:80
  33.6 3.2 %copy-start.1 = (bf16[512,384]{1,0:T(8,128)(2,1)S(1)}, bf16[512,384]{1,0:T(8,128)(2,1)}, u32[]{:S(2)}) copy-start(bf16[512,384]{1,0:T(8,128)(2,1)} %q_ref.3) | copy-start | bytes 1179652
  33.6 3.2 %copy-start.2 = (bf16[512,384]{1,0:T(8,128)(2,1)S(1)}, bf16[512,384]{1,0:T(8,128)(2,1)}, u32[]{:S(2)}) copy-start(bf16[512,384]{1,0:T(8,128)(2,1)} %k_ref.3) | copy-start | bytes 1179652
  33.7 3.2 %copy-start.3 = (bf16[512,384]{1,0:T(8,128)(2,1)S(1)}, bf16[512,384]{1,0:T(8,128)(2,1)}, u32[]{:S(2)}) copy-start(bf16[512,384]{1,0:T(8,128)(2,1)} %v_ref.3) | copy-start | bytes 1179652
  34.9 5.3 %collective-permute-start.4 = (bf16[4,64,2560]{2,1,0:T(8,128)(2,1)}, bf16[4,64,2560]{2,1,0:T(8,128)(2,1)}, u32[]{:S(2)}, u32[]{:S(2)}) collective-permute-start(bf16[4,64,2560]{2,1,0:T(8,128)(2,1)} %broadcast_select_fusion), channel_id=1, source_target_pairs={{0,1},{1,0},{2,3},{3,2},{4,5},{5,4},{6,7},{7,6},{8,9},{9,8},{10,11... | collective-permute-start | bytes 3932168 | tf_op jit(solution)/shard_map/ppermute | solution.py:84
  45.2 35.4 %all-to-all-start = ((bf16[16,4,40,384]{3,2,1,0:T(8,128)(2,1)}), bf16[16,4,40,384]{3,2,1,0:T(8,128)(2,1)}, u32[]{:S(2)}, u32[]{:S(2)}) async-start(bf16[16,4,40,384]{3,2,1,0:T(8,128)(2,1)} %copy.11), calls=%async_computation | async-start | bytes 3932160 | tf_op jit(solution)/shard_map/all_to_all | solution.py:101
  83.1 33.2 %collective-permute-start.7 = (bf16[40,384]{1,0:T(8,128)(2,1)}, bf16[40,384]{1,0:T(8,128)(2,1)}, u32[]{:S(2)}, u32[]{:S(2)}) collective-permute-start(bf16[40,384]{1,0:T(8,128)(2,1)} %get-tuple-element.13), channel_id=1, source_target_pairs={{0,384},{128,0},{256,128},{384,256},{1,385},{129,1},{257,129},{385... | collective-permute-start | bytes 92168 | tf_op jit(solution)/shard_map/ppermute | solution.py:107
  95.2 21.1 %collective-permute-start.6 = (bf16[40,384]{1,0:T(8,128)(2,1)}, bf16[40,384]{1,0:T(8,128)(2,1)}, u32[]{:S(2)}, u32[]{:S(2)}) collective-permute-start(bf16[40,384]{1,0:T(8,128)(2,1)} %get-tuple-element.14), channel_id=1, source_target_pairs={{0,128},{128,256},{256,384},{384,0},{1,129},{129,257},{257,385},{3... | collective-permute-start | bytes 92168 | tf_op jit(solution)/shard_map/ppermute | solution.py:107
  97.2 19.2 %collective-permute-start.5 = (bf16[40,384]{1,0:T(8,128)(2,1)}, bf16[40,384]{1,0:T(8,128)(2,1)}, u32[]{:S(2)}, u32[]{:S(2)}) collective-permute-start(bf16[40,384]{1,0:T(8,128)(2,1)} %get-tuple-element.12), channel_id=1, source_target_pairs={{0,256},{128,384},{256,0},{384,128},{1,257},{129,385},{257,1},{385... | collective-permute-start | bytes 92168 | tf_op jit(solution)/shard_map/ppermute | solution.py:107
  108.0 1.5 %copy-start = (bf16[2560,384]{1,0:T(8,128)(2,1)S(1)}, bf16[2560,384]{1,0:T(8,128)(2,1)}, u32[]{:S(2)}) copy-start(bf16[2560,384]{1,0:T(8,128)(2,1)} %w_ref.1) | copy-start | bytes 5898244
  109.6 1.0 copy-start.4

commit v2 on v1

v2 whole, which is shorter than its diff:
```python
import math

import jax
import jax.numpy as jnp
import numpy as np
from jax import lax
from jax.experimental import pallas as pl
from jax.experimental.pallas import tpu as pltpu
from jax.sharding import Mesh, PartitionSpec as P

HEAD = 128
LENGTH = 256
SCALING = 1.0 / math.sqrt(HEAD)
F32 = jnp.float32
BF16 = jnp.bfloat16
AXES = ("zh", "x", "y", "zl", "core")


def dot(a, b, ca, cb):
    return lax.dot_general(a, b, (((ca,), (cb,)), ((), ())), preferred_element_type=F32)


def head_probs(q, k):
    scores = dot(q, k, 1, 1) * SCALING
    n = scores.shape[0]
    causal = lax.broadcasted_iota(jnp.int32, (n, n), 0) >= lax.broadcasted_iota(
        jnp.int32, (n, n), 1
    )
    scores = jnp.where(causal, scores, -jnp.inf)
    row_max = jnp.max(scores, axis=1, keepdims=True)
    exp_scores = jnp.exp(scores - row_max)
    return exp_scores * (1.0 / jnp.sum(exp_scores, axis=1, keepdims=True))


def tiles(shape):
    for s in range(shape[0] // LENGTH):
        for h in range(shape[1] // HEAD):
            yield (pl.ds(s * LENGTH, LENGTH), pl.ds(h * HEAD, HEAD))


def attended_kernel(own_ref, q_ref, k_ref, v_ref, out_ref, kept_ref, sem):
    copy = pltpu.make_async_copy(own_ref, kept_ref, sem)
    copy.start()
    for at in tiles(out_ref.shape):
        probs = head_probs(q_ref[at], k_ref[at])
        out_ref[at] = dot(probs.astype(BF16), v_ref[at], 1, 0).astype(BF16)
    copy.wait()


def assemble(place_ref, pieces, rows_ref):
    zl, core = place_ref[0], place_ref[1]
    for at, (own, near, far, inner, outer) in ((core, pieces[:5]), (1 - core, pieces[5:])):
        rows_ref[zl, at] = own[...]
        rows_ref[zl ^ 1, at] = near[...]
        rows_ref[zl ^ 2, at] = far[...]
        rows_ref[zl ^ 3, at] = inner[...] + outer[...]
    return rows_ref[...].reshape(-1, rows_ref.shape[3])


def weight_kernel(place_ref, *refs):
    attended_ref, out_ref, kept_ref, rows_ref, sem = refs[10:]
    xy, zh, n, width = out_ref.shape
    rows = assemble(place_ref, refs[:10], rows_ref)
    keep = pltpu.make_async_copy(rows_ref, kept_ref, sem)
    keep.start()
    part = dot(rows, attended_ref[...], 0, 0).astype(BF16).reshape(zh, xy, n, width)
    for i in range(zh):
        out_ref[:, i] = part[i]
    keep.wait()


def sum_kernel(got_ref, out_ref):
    total = got_ref[0].astype(F32)
    for i in range(1, got_ref.shape[0]):
        total += got_ref[i].astype(F32)
    out_ref[...] = total.astype(out_ref.dtype)


def mean_kernel(scale, got_ref, out_ref):
    total = got_ref[0].astype(F32)
    for i in range(1, got_ref.shape[0]):
        total += got_ref[i].astype(F32)
    out_ref[...] = total * scale


def backward_kernel(rows_ref, *refs):
    ins, (gq_ref, gk_ref, gv_ref), (q_ref, k_ref, w_ref, v_ref), probs_ref, g_ref, sems = (
        refs[:4],
        refs[4:7],
        refs[7:11],
        refs[11],
        refs[12],
        refs[13],
    )
    copies = [
        pltpu.make_async_copy(a, b, sems.at[i])
        for i, (a, b) in enumerate(zip(ins, (q_ref, k_ref, w_ref, v_ref)))
    ]
    for copy in copies:
        copy.start()
    copies[0].wait()
    copies[1].wait()
    for i, at in enumerate(tiles(gq_ref.shape)):
        probs_ref[i] = head_probs(q_ref[at], k_ref[at])
    copies[2].wait()
    g_ref[...] = dot(rows_ref[...], w_ref[...], 1, 0).astype(BF16)
    copies[3].wait()
    for i, at in enumerate(tiles(gq_ref.shape)):
        q, k, v, g = q_ref[at], k_ref[at], v_ref[at], g_ref[at]
        probs = probs_ref[i]
        gv_ref[at] = dot(probs.astype(BF16), g, 0, 0).astype(BF16)
        grad_probs = dot(g, v, 1, 1)
        row_total = jnp.sum(probs * grad_probs, axis=1, keepdims=True)
        grad_scores = (probs * (grad_probs - row_total) * SCALING).astype(BF16)
        gq_ref[at] = dot(grad_scores, k, 1, 0).astype(BF16)
        gk_ref[at] = dot(grad_scores, q, 0, 0).astype(BF16)


def call(kernel, name, outs, *args, mib=48, spaces=(), out_spaces=None, scratch=()):
    vmem = pl.BlockSpec(memory_space=pltpu.VMEM)
    specs = [pl.BlockSpec(memory_space=m) for m in spaces] + [vmem] * (len(args) - len(spaces))
    many = isinstance(outs, tuple)
    return pl.pallas_call(
        kernel,
        out_shape=outs,
        in_specs=specs,
        out_specs=tuple(pl.BlockSpec(memory_space=m) for m in out_spaces or [pltpu.VMEM] * len(outs))
        if many
        else vmem,
        scratch_shapes=scratch,
        compiler_params=pltpu.CompilerParams(vmem_limit_bytes=mib * 2**20),
        name=name,
    )(*args)


def swap_cores(piece, zls=None):
    if zls is None:
        return lax.ppermute(piece, "core", [(0, 1), (1, 0)])
    pairs = [(2 * i + c, 2 * i + 1 - c) for i in zls for c in range(2)]
    return lax.ppermute(piece, ("zl", "core"), pairs)


def on_device(queries, key_rows, value_rows, out_weight, grad_out):
    shape = queries.shape
    width = shape[1]
    d = out_weight.shape[0]
    n_dp = lax.axis_size("zh") * lax.axis_size("x") * lax.axis_size("y")
    n_zh = lax.axis_size("zh")
    n_zl = lax.axis_size("zl")
    r = grad_out.shape[0]
    same = jax.ShapeDtypeStruct(shape, BF16)
    place = jnp.stack([lax.axis_index("zl"), lax.axis_index("core")]).astype(jnp.int32)

    own = grad_out
    far = lax.ppermute(own, "zl", [(0, 2), (2, 0), (1, 3), (3, 1)])
    inner = lax.ppermute(own, "zl", [(1, 2), (2, 1)])
    near = lax.ppermute(own, "zl", [(0, 1), (1, 0), (2, 3), (3, 2)])
    attended, own_kept = call(
        attended_kernel,
        "attended",
        (same, jax.ShapeDtypeStruct(own.shape, BF16)),
        pltpu.with_memory_space_constraint(own, pltpu.HBM),
        queries,
        key_rows,
        value_rows,
        spaces=[pltpu.HBM],
        scratch=[pltpu.SemaphoreType.DMA],
    )
    own_over = swap_cores(own)
    far, attended, own_over = lax.optimization_barrier((far, attended, own_over))
    outer = lax.ppermute(far, "zl", [(1, 0), (2, 3)])
    pieces = (
        own_kept,
        near,
        far,
        inner,
        outer,
        own_over,
        swap_cores(near),
        swap_cores(far),
        swap_cores(inner, (1, 2)),
        swap_cores(outer, (0, 3)),
    )
    piece_spaces = [pltpu.SMEM]
    rows_scratch = pltpu.VMEM((n_zl, 2, r, d), BF16)
    part, rows = call(
        weight_kernel,
        "weight",
        (
            jax.ShapeDtypeStruct((n_dp // n_zh, n_zh, d // n_dp, width), BF16),
            jax.ShapeDtypeStruct(rows_scratch.shape, BF16),
        ),
        place,
        *pieces,
        attended,
        spaces=piece_spaces,
        out_spaces=[pltpu.VMEM, pltpu.HBM],
        scratch=[rows_scratch, pltpu.SemaphoreType.DMA],
    )
    got = lax.all_to_all(part, ("x", "y"), 0, 0, tiled=True)
    plane = call(sum_kernel, "sum", jax.ShapeDtypeStruct(got.shape[1:], BF16), got)
    rows, plane = lax.optimization_barrier((rows, plane))
    last = lax.all_to_all(plane, "zh", 0, 0, tiled=True)
    gq, gk, gv = call(
        backward_kernel,
        "backward",
        (same, same, same),
        rows.reshape(shape[0], d),
        *(
            pltpu.with_memory_space_constraint(a, pltpu.HBM)
            for a in (queries, key_rows, out_weight, value_rows)
        ),
        spaces=[pltpu.VMEM] + [pltpu.HBM] * 4,
        scratch=[
            pltpu.VMEM(shape, BF16),
            pltpu.VMEM(shape, BF16),
            pltpu.VMEM(out_weight.shape, BF16),
            pltpu.VMEM(shape, BF16),
            pltpu.VMEM((shape[0] // LENGTH * width // HEAD, LENGTH, LENGTH), F32),
            pltpu.VMEM(shape, BF16),
            pltpu.SemaphoreType.DMA((4,)),
        ],
    )
    grad_weight = call(
        lambda a, b: mean_kernel(1.0 / n_dp, a, b),
        "mean",
        jax.ShapeDtypeStruct(last.shape[1:], F32),
        last,
    )
    return gq, gk, gv, grad_weight


def solution(mesh):
    split = Mesh(np.asarray(mesh.devices).reshape(4, 4, 4, 4, 2), AXES)
    dp, tensor = ("zh", "x", "y"), ("zl", "core")
    return jax.shard_map(
        on_device,
        mesh=split,
        in_specs=(P(dp, tensor), P(dp, tensor), P(dp, tensor), P(None, tensor), P(AXES, None)),
        out_specs=(P(dp, tensor), P(dp, tensor), P(dp, tensor), P(dp, tensor)),
        check_vma=False,
    )
```

time: 118 us -> 102 us (0.86)
  blocking collectives: 0 us -> 32.8 us
  waiting for transfers between devices: 48.9 us -> 18.6 us
  starting transfers between devices: 46.4 us -> 33.3 us
  other arithmetic: 7.53 us -> 0.08 us
  Pallas kernels: 8.65 us -> 12.4 us
  local copies, waits for them, and re-layouts: 5.45 us -> 2.99 us
    all_to_all x0 -> x1, blocking collectives: none -> 32.8 us  [on_device(): got = lax.all_to_all(part, ('x', 'y'), 0, 0, tiled=True)]
    all_to_all x1, waiting for transfers between devices: 28 us -> 6.7 us  [on_device(): last = lax.all_to_all(plane, 'zh', 0, 0, tiled=True)]
    ppermute x8 -> x9, starting transfers between devices: 39 us -> 19.3 us  [the longest x3 5.75 us: swap_cores(): return lax.ppermute(piece, 'core', [(0, 1), (1, 0)])]
    ppermute x8 -> x9, waiting for transfers between devices: 20.8 us -> 11.9 us  [the longest x1 5 us: on_device(): far = lax.ppermute(own, 'zl', [(0, 2), (2, 0), (1, 3), (3, 1)])]
    all_to_all x1, starting transfers between devices: 7.39 us -> 14 us  [on_device(): last = lax.all_to_all(plane, 'zh', 0, 0, tiled=True)]
    pallas_call x3 -> x5, Pallas kernels: 8.65 us -> 12.4 us  [call(): pl.pallas_call(kernel, out_shape=outs, in_specs=specs, out_specs=tuple((p...]
    another operation x4 -> x1, other arithmetic: 2.98 us -> 0.08 us  [on_device(): jnp.stack([lax.axis_index('zl'), lax.axis_index('core')]).astype(jnp.int32)]
    reduce_sum x1 -> x0, other arithmetic: 1.83 us -> none  [on_device(): plane = jnp.sum(got.astype(F32), axis=0).astype(BF16)]
  transfers between devices with their start and end apart: 9 -> 10, of which waited for: 4 -> 5; matrix products, arithmetic and copies ran while one was open for 0% -> 0% of each run, Pallas kernels for 6% -> 8%
where the time goes in v2:
time: 102 us; the launch traced here: 101 us
  starting transfers between devices  33.3 us (33%)
  blocking collectives  32.8 us (32%)
  waiting for transfers between devices  18.6 us (18%)
  Pallas kernels  12.4 us (12%)
  local copies, waits for them, and re-layouts  2.99 us (3%)
    all_to_all x1, blocking collectives, on_device(): got = lax.all_to_all(part, ('x', 'y'), 0, 0, tiled=True)  32.8 us
    all_to_all x1, starting transfers between devices, on_device(): last = lax.all_to_all(plane, 'zh', 0, 0, tiled=True)  14 us
    pallas_call x5, Pallas kernels, call(): pl.pallas_call(kernel, out_shape=outs, in_specs=specs, out_specs=tuple((p...  12.4 us
    all_to_all x1, waiting for transfers between devices, on_device(): last = lax.all_to_all(plane, 'zh', 0, 0, tiled=True)  6.7 us
    ppermute x3, starting transfers between devices, swap_cores(): return lax.ppermute(piece, 'core', [(0, 1), (1, 0)])  5.75 us
    ppermute x1, starting transfers between devices, on_device(): far = lax.ppermute(own, 'zl', [(0, 2), (2, 0), (1, 3), (3, 1)])  5.18 us
    ppermute x1, waiting for transfers between devices, on_device(): far = lax.ppermute(own, 'zl', [(0, 2), (2, 0), (1, 3), (3, 1)])  5 us
    ppermute x1, waiting for transfers between devices, on_device(): outer = lax.ppermute(far, 'zl', [(1, 0), (2, 3)])  4.12 us
  transfers between devices with their start and end apart: 10, of which 5 were waited for; matrix products, arithmetic and copies ran while one was open for 0% of the time, Pallas kernels for 8%

profile of v2, /device:TPU:8, one launch (start us, length us, event | category | flops | bytes accessed | tf_op | source)
XLA Modules:
  0.0 101.0 jit_solution(16545077058339594415)
XLA Ops:
  0.6 5.2 %collective-permute-start.1 = (bf16[64,2560]{1,0:T(8,128)(2,1)}, bf16[64,2560]{1,0:T(8,128)(2,1)S(1)}, u32[]{:S(2)}, u32[]{:S(2)}) collective-permute-start(bf16[64,2560]{1,0:T(8,128)(2,1)} %own_ref.1), channel_id=1, source_target_pairs={{0,4},{4,0},{2,6},{6,2},{1,5},{5,1},{3,7},{7,3},{8,12},{12,8},{10,... | collective-permute-start | bytes 983048 | tf_op jit(solution)/shard_map/ppermute | solution.py:155
  5.8 1.9 %collective-permute-start.2 = (bf16[64,2560]{1,0:T(8,128)(2,1)}, bf16[64,2560]{1,0:T(8,128)(2,1)S(1)}, u32[]{:S(2)}, u32[]{:S(2)}) collective-permute-start(bf16[64,2560]{1,0:T(8,128)(2,1)} %own_ref.1), channel_id=1, source_target_pairs={{0,1},{1,0},{2,3},{3,2},{4,5},{5,4},{6,7},{7,6},{8,9},{9,8},{10,11... | collective-permute-start | bytes 983048 | tf_op jit(solution)/shard_map/ppermute | solution.py:138
  7.7 3.8 %collective-permute-start = (bf16[64,2560]{1,0:T(8,128)(2,1)}, bf16[64,2560]{1,0:T(8,128)(2,1)S(1)}, u32[]{:S(2)}, u32[]{:S(2)}) collective-permute-start(bf16[64,2560]{1,0:T(8,128)(2,1)} %own_ref.1), channel_id=1, source_target_pairs={{0,2},{2,0},{4,6},{6,4},{1,3},{3,1},{5,7},{7,5},{8,10},{10,8},{12,... | collective-permute-start | bytes 983048 | tf_op jit(solution)/shard_map/ppermute | solution.py:157
  11.6 0.7 collective-permute-start.3
  12.3 0.0 copy-start.1
  12.3 1.0 copy-done.1
  13.3 0.0 copy-start.2
  13.3 1.0 copy-done.2
  14.3 0.0 copy-start.3
  14.3 1.0 copy-done.3
  15.3 1.3 %attended.1 = (bf16[512,384]{1,0:T(8,128)(2,1)S(1)}, bf16[64,2560]{1,0:T(8,128)(2,1)S(1)}) custom-call(bf16[64,2560]{1,0:T(8,128)(2,1)} %own_ref.1, bf16[512,384]{1,0:T(8,128)(2,1)S(1)} %copy-done.1, bf16[512,384]{1,0:T(8,128)(2,1)S(1)} %copy-done.2, bf16[512,384]{1,0:T(8,128)(2,1)S(1)} %copy-done.3), custom_call_target="tpu_custom_call" | custom-call | tf_op jit(solution)/shard_map/attended/pallas_call | solution.py:123
  16.6 5.0 %collective-permute-done.1.refs_2_ = bf16[64,2560]{1,0:T(8,128)(2,1)S(1)} collective-permute-done((bf16[64,2560]{1,0:T(8,128)(2,1)}, bf16[64,2560]{1,0:T(8,128)(2,1)S(1)}, u32[]{:S(2)}, u32[]{:S(2)}) %collective-permute-start.1) | collective-permute-done | bytes 327712 | tf_op jit(solution)/shard_map/ppermute | solution.py:155
  21.6 0.0 collective-permute-done.2.refs_5_
  21.6 1.3 %collective-permute-start.4 = (bf16[64,2560]{1,0:T(8,128)(2,1)S(1)}, bf16[64,2560]{1,0:T(8,128)(2,1)S(1)}, u32[]{:S(2)}, u32[]{:S(2)}) collective-permute-start(bf16[64,2560]{1,0:T(8,128)(2,1)S(1)} %collective-permute-done.1.refs_2_), channel_id=1, source_target_pairs={{2,0},{4,6},{3,1},{5,7},{10,8},{12,14},{11,9},{13,15},{18,16},{20,... | collective-permute-start | bytes 983048 | tf_op jit(solution)/shard_map/ppermute | solution.py:171
  22.9 1.9 %collective-permute-start.6 = (bf16[64,2560]{1,0:T(8,128)(2,1)S(1)}, bf16[64,2560]{1,0:T(8,128)(2,1)S(1)}, u32[]{:S(2)}, u32[]{:S(2)}) collective-permute-start(bf16[64,2560]{1,0:T(8,128)(2,1)S(1)} %collective-permute-done.1.refs_2_), channel_id=1, source_target_pairs={{0,1},{1,0},{2,3},{3,2},{4,5},{5,4},{6,7},{7,6},{8,9},{9,8},{10,11... | collective-permute-start | bytes 983048 | tf_op jit(solution)/shard_map/ppermute | solution.py:138
  24.8 1.2 %collective-permute-done.refs_1_ = bf16[64,2560]{1,0:T(8,128)(2,1)S(1)} collective-permute-done((bf16[64,2560]{1,0:T(8,128)(2,1)}, bf16[64,2560]{1,0:T(8,128)(2,1)S(1)}, u32[]{:S(2)}, u32[]{:S(2)}) %collective-permute-start) | collective-permute-done | bytes 327712 | tf_op jit(solution)/shard_map/ppermute | solution.py:157
  26.0 1.9 %collective-permute-start.5 = (bf16[64,2560]{1,0:T(8,128)(2,1)S(1)}, bf16[64,2560]{1,0:T(8,128)(2,1)S(1)}, u32[]{:S(2)}, u32[]{:S(2)}) collective-permute-start(bf16[64,2560]{1,0:T(8,128)(2,1)S(1)} %collective-permute-done.refs_1_), channel_id=1, source_target_pairs={{0,1},{1,0},{2,3},{3,2},{4,5},{5,4},{6,7},{7,6},{8,9},{9,8},{10,11... | collective-permute-start | bytes 983048 | tf_op jit(solution)/shard_map/ppermute | solution.py:138
  27.9 0.0 collective-permute-done.3.refs_3_
  27.9 0.7 collective-permute-start.7
  28.6 4.1 %collective-permute-done.4.refs_4_ = bf16[64,2560]{1,0:T(8,128)(2,1)S(1)} collective-permute-done((bf16[64,2560]{1,0:T(8,128)(2,1)S(1)}, bf16[64,2560]{1,0:T(8,128)(2,1)S(1)}, u32[]{:S(2)}, u32[]{:S(2)}) %collective-permute-start.4) | collective-permute-done | bytes 327712 | tf_op jit(solution)/shard_map/ppermute | solution.py:171
  32.7 1.9 %collective-permute-start.8 = (bf16[64,2560]{1,0:T(8,128)(2,1)S(1)}, bf16[64,2560]{1,0:T(8,128)(2,1)}, u32[]{:S(2)}, u32[]{:S(2)}) collective-permute-start(bf16[64,2560]{1,0:T(8,128)(2,1)S(1)} %collective-permute-done.4.refs_4_), channel_id=1, source_target_pairs={{0,1},{1,0},{6,7},{7,6},{8,9},{9,8},{14,15},{15,14},{16,17},{17,16... | collective-permute-start | bytes 983048 | tf_op jit(solution)/shard_map/ppermute | solution.py:140
  34.7 0.1 pad_add_fusion.place_ref
  34.7 0.0 collective-permute-done.5.refs_6_
  34.7 0.0 collective-permute-done.7.refs_8_
  34.7 0.0 collective-permute-done.6.refs_7_
  34.7 1.6 %collective-permute-done.8.refs_9_ = bf16[64,2560]{1,0:T(8,128)(2,1)} collective-permute-done((bf16[64,2560]{1,0:T(8,128)(2,1)S(1)}, bf16[64,2560]{1,0:T(8,128)(2,1)}, u32[]{:S(2)}, u32[]{:S(2)}) %collective-permute-start.8) | collective-permute-done | bytes 327712 | tf_op jit(solution)/shard_map/ppermute | solution.py:140
  36.4 2.7 %weight.1 = (bf16[16,4,40,384]{3,2,1,0:T(8,128)(2,1)S(1)}, bf16[4,2,64,2560]{3,2,1,0:T(8,128)(2,1)}) custom-call(s32[2]{0:T(128)S(1)} %pad_add_fusion.place_ref, bf16[64,2560]{1,0:T(8,128)(2,1)S(1)} %get-tuple-element.16.refs_0_, bf16[64,2560]{1,0:T(8,128)(2,1)S(1)} %collective-permute-done.refs_1_, bf16[64,2560]{1,0:T(8,128)(2,1)S(1)} %collective-permute-done.1.refs_2_, ...), custom_call_target="tpu_custom_call" | custom-call | tf_op jit(solution)/shard_map/weight/pallas_call | solution.py:123
  39.1 0.0 copy-start
  39.1 32.8 %all_to_all.10.got_ref = bf16[16,4,40,384]{3,2,1,0:T(8,128)(2,1)S(1)} all-to-all(bf16[16,4,40,384]{3,2,1,0:T(8,128)(2,1)S(1)} %get-tuple-element.22), channel_id=1, replica_groups=mesh['zh'=4,'x'=4,'y'=4,'zl'=4,'core'=2] {'x','y'}, dimensions={0} | all-to-all | bytes 3932160 | tf_op jit(solution)/shard_map/all_to_all | solution.py:200
  71.9 0.9 sum.1
  72.9 14.0 %all-to-all-start.1 = ((bf16[4,40,384]{2,1,0:T(8,128)(2,1)}), bf16[4,40,384]{2,1,0:T(8,128)(2,1)S(1)}, u32[]{:S(2)}, u32[]{:S(2)}) async-start(bf16[4,40,384]{2,1,0:T(8,128)(2,1)} %sum.1), calls=%async_computation.1 | async-start | bytes 245760 | tf_op jit(solution)/shard_map/all_to_all | solution.py:203
  86.9 0.0 copy-done
  86.9 6.8 %backward.1 = (bf16[512,384]{1,0:T(8,128)(2,1)}, bf16[512,384]{1,0:T(8,128)(2,1)}, bf16[512,384]{1,0:T(8,128)(2,1)}) custom-call(bf16[512,2560]{1,0:T(8,128)(2,1)S(1)} %bitcast.3, bf16[512,384]{1,0:T(8,128)(2,1)} %refs_0_.1, bf16[512,384]{1,0:T(8,128)(2,1)} %refs_1_.1, bf16[2560,384]{1,0:T(8,128)(2,1)} %refs_2_.1, bf16[512,384]{1,0:T(8,128)(2,1)} %refs_3_.1), custom_call_target="tpu_custom_call" | custom-call | tf_op jit(solution)/shard_map/backward/pallas_call | solution.py:123
  93.6 6.7 %all-to-all-done.1.a = bf16[4,40,384]{2,1,0:T(8,128)(2,1)S(1)} async-done(((bf16[4,40,384]{2,1,0:T(8,128)(2,1)}), bf16[4,40,384]{2,1,0:T(8,128)(2,1)S(1)}, u32[]{:S(2)}, u32[]{:S(2)}) %all-to-all-start.1) | async-done | bytes 122912 | tf_op jit(solution)/shard_map/all_to_all | solution.py:203
  100.3 0.6 mean.1
Async XLA Ops:
  0.6 21.0 %collective-permute-start.1 = (bf16[64,2560]{1,0:T(8,128)(2,1)}, bf16[64,2560]{1,0:T(8,128)(2,1)S(1)}, u32[]{:S(2)}, u32[]{:S(2)}) collective-permute-start(bf16[64,2560]{1,0:T(8,128)(2,1)} %own_ref.1), channel_id=1, source_target_pairs={{0,4},{4,0},{2,6},{6,2},{1,5},{5,1},{3,7},{7,3},{8,12},{12,8},{10,... | collective-permute-start | bytes 983048 | tf_op jit(solution)/shard_map/ppermute | solution.py:155
  5.8 15.8 %collective-permute-start.2 = (bf16[64,2560]{1,0:T(8,128)(2,1)}, bf16[64,2560]{1,0:T(8,128)(2,1)S(1)}, u32[]{:S(2)}, u32[]{:S(2)}) collective-permute-start(bf16[64,2560]{1,0:T(8,128)(2,1)} %own_ref.1), channel_id=1, source_target_pairs={{0,1},{1,0},{2,3},{3,2},{4,5},{5,4},{6,7},{7,6},{8,9},{9,8},{10,11... | collective-permute-start | bytes 983048 | tf_op jit(solution)/shard_map/ppermute | solution.py:138
  7.7 18.3 %collective-permute-start = (bf16[64,2560]{1,0:T(8,128)(2,1)}, bf16[64,2560]{1,0:T(8,128)(2,1)S(1)}, u32[]{:S(2)}, u32[]{:S(2)}) collective-permute-start(bf16[64,2560]{1,0:T(8,128)(2,1)} %own_ref.1), channel_id=1, source_target_pairs={{0,2},{2,0},{4,6},{6,4},{1,3},{3,1},{5,7},{7,5},{8,10},{10,8},{12,... | collective-permute-start | bytes 983048 | tf_op jit(solution)/shard_map/ppermute | solution.py:157
  11.6 16.3 %collective-permute-start.3 = (bf16[64,2560]{1,0:T(8,128)(2,1)}, bf16[64,2560]{1,0:T(8,128)(2,1)S(1)}, u32[]{:S(2)}, u32[]{:S(2)}) collective-permute-start(bf16[64,2560]{1,0:T(8,128)(2,1)} %own_ref.1), channel_id=1, source_target_pairs={{2,4},{4,2},{3,5},{5,3},{10,12},{12,10},{11,13},{13,11},{18,20},{2... | collective-permute-start | bytes 983048 | tf_op jit(solution)/shard_map/ppermute | solution.py:156
  12.3 1.0 copy-start.1
  13.3 1.0 copy-start.2
  14.3 1.0 copy-start.3
  21.6 11.1 %collective-permute-start.4 = (bf16[64,2560]{1,0:T(8,128)(2,1)S(1)}, bf16[64,2560]{1,0:T(8,128)(2,1)S(1)}, u32[]{:S(2)}, u32[]{:S(2)}) collective-permute-start(bf16[64,2560]{1,0:T(8,128)(2,1)S(1)} %collective-permute-done.1.refs_2_), channel_id=1, source_target_pairs={{2,0},{4,6},{3,1},{5,7},{10,8},{12,14},{11,9},{13,15},{18,16},{20,... | collective-permute-start | bytes 983048 | tf_op jit(solution)/shard_map/ppermute | solution.py:171
  22.9 11.8 %collective-permute-start.6 = (bf16[64,2560]{1,0:T(8,128)(2,1)S(1)}, bf16[64,2560]{1,0:T(8,128)(2,1)S(1)}, u32[]{:S(2)}, u32[]{:S(2)}) collective-permute-start(bf16[64,2560]{1,0:T(8,128)(2,1)S(1)} %collective-permute-done.1.refs_2_), channel_id=1, source_target_pairs={{0,1},{1,0},{2,3},{3,2},{4,5},{5,4},{6,7},{7,6},{8,9},{9,8},{10,11... | collective-permute-start | bytes 983048 | tf_op jit(solution)/shard_map/ppermute | solution.py:138
  26.0 8.7 %collective-permute-start.5 = (bf16[64,2560]{1,0:T(8,128)(2,1)S(1)}, bf16[64,2560]{1,0:T(8,128)(2,1)S(1)}, u32[]{:S(2)}, u32[]{:S(2)}) collective-permute-start(bf16[64,2560]{1,0:T(8,128)(2,1)S(1)} %collective-permute-done.refs_1_), channel_id=1, source_target_pairs={{0,1},{1,0},{2,3},{3,2},{4,5},{5,4},{6,7},{7,6},{8,9},{9,8},{10,11... | collective-permute-start | bytes 983048 | tf_op jit(solution)/shard_map/ppermute | solution.py:138
  27.9 6.8 %collective-permute-start.7 = (bf16[64,2560]{1,0:T(8,128)(2,1)S(1)}, bf16[64,2560]{1,0:T(8,128)(2,1)S(1)}, u32[]{:S(2)}, u32[]{:S(2)}) collective-permute-start(bf16[64,2560]{1,0:T(8,128)(2,1)S(1)} %collective-permute-done.3.refs_3_), channel_id=1, source_target_pairs={{2,3},{3,2},{4,5},{5,4},{10,11},{11,10},{12,13},{13,12},{18,19},{1... | collective-permute-start | bytes 983048 | tf_op jit(solution)/shard_map/ppermute | solution.py:140
  32.7 3.6 %collective-permute-start.8 = (bf16[64,2560]{1,0:T(8,128)(2,1)S(1)}, bf16[64,2560]{1,0:T(8,128)(2,1)}, u32[]{:S(2)}, u32[]{:S(2)}) collective-permute-start(bf16[64,2560]{1,0:T(8,128)(2,1)S(1)} %collective-permute-done.4.refs_4_), channel_id=1, source_target_pairs={{0,1},{1,0},{6,7},{7,6},{8,9},{9,8},{14,15},{15,14},{16,17},{17,16... | collective-permute-start | bytes 983048 | tf_op jit(solution)/shard_map/ppermute | solution.py:140
  39.1 47.7 %copy-start = (bf16[4,2,64,2560]{3,2,1,0:T(8,128)(2,1)S(1)}, bf16[4,2,64,2560]{3,2,1,0:T(8,128)(2,1)}, u32[]{:S(2)}) copy-start(bf16[4,2,64,2560]{3,2,1,0:T(8,128)(2,1)} %get-tuple-element.23) | copy-start | bytes 7864324
  72.9 27.5 %all-to-all-start.1 = ((bf16[4,40,384]{2,1,0:T(8,128)(2,1)}), bf16[4,40,384]{2,1,0:T(8,128)(2,1)S(1)}, u32[]{:S(2)}, u32[]{:S(2)}) async-start(bf16[4,40,384]{2,1,0:T(8,128)(2,1)} %sum.1), calls=%async_computation.1 | async-start | bytes 245760 | tf_op jit(solution)/shard_map/all_to_all | solution.py:203

commit v3 on v2

--- a/solution.py
+++ b/solution.py
@@ -20,11 +20,15 @@
     return lax.dot_general(a, b, (((ca,), (cb,)), ((), ())), preferred_element_type=F32)
 
 
-def head_probs(q, k):
-    scores = dot(q, k, 1, 1) * SCALING
-    n = scores.shape[0]
-    causal = lax.broadcasted_iota(jnp.int32, (n, n), 0) >= lax.broadcasted_iota(
-        jnp.int32, (n, n), 1
+ORDER_ZH = [2, 3, 0, 1]
+ORDER_XY = [10, 11, 8, 9, 14, 15, 12, 13, 2, 3, 0, 1, 6, 7, 4, 5]
+HALVES = ((0, LENGTH // 2), (LENGTH // 2, LENGTH))
+
+
+def half_probs(q, k, at, end):
+    scores = dot(q[at:end], k[:end], 1, 1) * SCALING
+    causal = at + lax.broadcasted_iota(jnp.int32, scores.shape, 0) >= lax.broadcasted_iota(
+        jnp.int32, scores.shape, 1
     )
     scores = jnp.where(causal, scores, -jnp.inf)
     row_max = jnp.max(scores, axis=1, keepdims=True)
@@ -32,19 +36,32 @@
     return exp_scores * (1.0 / jnp.sum(exp_scores, axis=1, keepdims=True))
 
 
+def widened(first, second):
+    none = jnp.zeros((first.shape[0], second.shape[1] - first.shape[1]), first.dtype)
+    return jnp.concatenate([jnp.concatenate([first, none], axis=1), second], axis=0)
+
+
 def tiles(shape):
     for s in range(shape[0] // LENGTH):
         for h in range(shape[1] // HEAD):
             yield (pl.ds(s * LENGTH, LENGTH), pl.ds(h * HEAD, HEAD))
 
 
-def attended_kernel(own_ref, q_ref, k_ref, v_ref, out_ref, kept_ref, sem):
-    copy = pltpu.make_async_copy(own_ref, kept_ref, sem)
-    copy.start()
+def fetch(sources, targets, sems):
+    copies = [pltpu.make_async_copy(a, b, sems.at[i]) for i, (a, b) in enumerate(zip(sources, targets))]
+    for copy in copies:
+        copy.start()
+    return copies
+
+
+def attended_kernel(*refs):
+    ins, (out_ref, own_ref, q_ref, k_ref, v_ref, sems) = refs[:4], refs[4:]
+    for copy in fetch(ins, (q_ref, k_ref, v_ref, own_ref), sems):
+        copy.wait()
     for at in tiles(out_ref.shape):
-        probs = head_probs(q_ref[at], k_ref[at])
-        out_ref[at] = dot(probs.astype(BF16), v_ref[at], 1, 0).astype(BF16)
-    copy.wait()
+        q, k = q_ref[at], k_ref[at]
+        probs = widened(*(half_probs(q, k, *half).astype(BF16) for half in HALVES))
+        out_ref[at] = dot(probs, v_ref[at], 1, 0).astype(BF16)
 
 
 def assemble(place_ref, pieces, rows_ref):
@@ -65,7 +82,8 @@
     keep.start()
     part = dot(rows, attended_ref[...], 0, 0).astype(BF16).reshape(zh, xy, n, width)
     for i in range(zh):
-        out_ref[:, i] = part[i]
+        for j, block in enumerate(ORDER_XY):
+            out_ref[j, i] = part[i, block]
     keep.wait()
 
 
@@ -73,7 +91,8 @@
     total = got_ref[0].astype(F32)
     for i in range(1, got_ref.shape[0]):
         total += got_ref[i].astype(F32)
-    out_ref[...] = total.astype(out_ref.dtype)
+    for i, block in enumerate(ORDER_ZH):
+        out_ref[i] = total[block].astype(out_ref.dtype)
 
 
 def mean_kernel(scale, got_ref, out_ref):
@@ -84,34 +103,29 @@
 
 
 def backward_kernel(rows_ref, *refs):
-    ins, (gq_ref, gk_ref, gv_ref), (q_ref, k_ref, w_ref, v_ref), probs_ref, g_ref, sems = (
-        refs[:4],
-        refs[4:7],
-        refs[7:11],
-        refs[11],
-        refs[12],
-        refs[13],
-    )
-    copies = [
-        pltpu.make_async_copy(a, b, sems.at[i])
-        for i, (a, b) in enumerate(zip(ins, (q_ref, k_ref, w_ref, v_ref)))
-    ]
-    for copy in copies:
-        copy.start()
+    ins, (gq_ref, gk_ref, gv_ref) = refs[:4], refs[4:7]
+    q_ref, k_ref, w_ref, v_ref, first_ref, second_ref, g_ref, sems = refs[7:]
+    copies = fetch(ins, (q_ref, k_ref, w_ref, v_ref), sems)
     copies[0].wait()
     copies[1].wait()
     for i, at in enumerate(tiles(gq_ref.shape)):
-        probs_ref[i] = head_probs(q_ref[at], k_ref[at])
+        q, k = q_ref[at], k_ref[at]
+        for ref, half in zip((first_ref, second_ref), HALVES):
+            ref[i] = half_probs(q, k, *half)
     copies[2].wait()
     g_ref[...] = dot(rows_ref[...], w_ref[...], 1, 0).astype(BF16)
     copies[3].wait()
     for i, at in enumerate(tiles(gq_ref.shape)):
         q, k, v, g = q_ref[at], k_ref[at], v_ref[at], g_ref[at]
-        probs = probs_ref[i]
-        gv_ref[at] = dot(probs.astype(BF16), g, 0, 0).astype(BF16)
-        grad_probs = dot(g, v, 1, 1)
-        row_total = jnp.sum(probs * grad_probs, axis=1, keepdims=True)
-        grad_scores = (probs * (grad_probs - row_total) * SCALING).astype(BF16)
+        probs_low, grad_scores = [], []
+        for ref, (start, end) in zip((first_ref, second_ref), HALVES):
+            probs = ref[i]
+            grad_probs = dot(g[start:end], v[:end], 1, 1)
+            row_total = jnp.sum(probs * grad_probs, axis=1, keepdims=True)
+            probs_low.append(probs.astype(BF16))
+            grad_scores.append((probs * (grad_probs - row_total) * SCALING).astype(BF16))
+        probs_low, grad_scores = widened(*probs_low), widened(*grad_scores)
+        gv_ref[at] = dot(probs_low, g, 0, 0).astype(BF16)
         gq_ref[at] = dot(grad_scores, k, 1, 0).astype(BF16)
         gk_ref[at] = dot(grad_scores, q, 0, 0).astype(BF16)
 
@@ -155,16 +169,17 @@
     far = lax.ppermute(own, "zl", [(0, 2), (2, 0), (1, 3), (3, 1)])
     inner = lax.ppermute(own, "zl", [(1, 2), (2, 1)])
     near = lax.ppermute(own, "zl", [(0, 1), (1, 0), (2, 3), (3, 2)])
+    n_tiles = shape[0] // LENGTH * width // HEAD
     attended, own_kept = call(
         attended_kernel,
         "attended",
         (same, jax.ShapeDtypeStruct(own.shape, BF16)),
-        pltpu.with_memory_space_constraint(own, pltpu.HBM),
-        queries,
-        key_rows,
-        value_rows,
-        spaces=[pltpu.HBM],
-        scratch=[pltpu.SemaphoreType.DMA],
+        *(
+            pltpu.with_memory_space_constraint(a, pltpu.HBM)
+            for a in (queries, key_rows, value_rows, own)
+        ),
+        spaces=[pltpu.HBM] * 4,
+        scratch=[pltpu.VMEM(shape, BF16)] * 3 + [pltpu.SemaphoreType.DMA((4,))],
     )
     own_over = swap_cores(own)
     far, attended, own_over = lax.optimization_barrier((far, attended, own_over))
@@ -197,10 +212,10 @@
         out_spaces=[pltpu.VMEM, pltpu.HBM],
         scratch=[rows_scratch, pltpu.SemaphoreType.DMA],
     )
-    got = lax.all_to_all(part, ("x", "y"), 0, 0, tiled=True)
+    got = lax.all_to_all(part, ("x", "y"), 0, 0, axis_index_groups=[ORDER_XY], tiled=True)
     plane = call(sum_kernel, "sum", jax.ShapeDtypeStruct(got.shape[1:], BF16), got)
     rows, plane = lax.optimization_barrier((rows, plane))
-    last = lax.all_to_all(plane, "zh", 0, 0, tiled=True)
+    last = lax.all_to_all(plane, "zh", 0, 0, axis_index_groups=[ORDER_ZH], tiled=True)
     gq, gk, gv = call(
         backward_kernel,
         "backward",
@@ -216,7 +231,7 @@
             pltpu.VMEM(shape, BF16),
             pltpu.VMEM(out_weight.shape, BF16),
             pltpu.VMEM(shape, BF16),
-            pltpu.VMEM((shape[0] // LENGTH * width // HEAD, LENGTH, LENGTH), F32),
+            *(pltpu.VMEM((n_tiles, end - at, end), F32) for at, end in HALVES),
             pltpu.VMEM(shape, BF16),
             pltpu.SemaphoreType.DMA((4,)),
         ],

time: 102 us -> 95.1 us (0.932)
  waiting for transfers between devices: 18.6 us -> 13.9 us
  local copies, waits for them, and re-layouts: 2.99 us -> 0.01 us
  starting transfers between devices: 33.3 us -> 35.4 us
  blocking collectives: 32.8 us -> 31.5 us
    all_to_all x1, waiting for transfers between devices: 6.7 us -> 0.01 us  [on_device(): lax.all_to_all(plane, 'zh', 0, 0, axis_index_groups=[ORDER_ZH], tiled=True)]
    unnamed x8 -> x2, local copies, waits for them, and re-layouts: 2.99 us -> 0.01 us
    all_to_all x1, starting transfers between devices: 14 us -> 16.1 us  [on_device(): lax.all_to_all(plane, 'zh', 0, 0, axis_index_groups=[ORDER_ZH], tiled=True)]
    ppermute x1, waiting for transfers between devices: 5 us -> 6.99 us  [on_device(): far = lax.ppermute(own, 'zl', [(0, 2), (2, 0), (1, 3), (3, 1)])]
    all_to_all x1, blocking collectives: 32.8 us -> 31.5 us  [on_device(): lax.all_to_all(part, ('x', 'y'), 0, 0, axis_index_groups=[ORDER_XY], tile...]
  transfers between devices with their start and end apart: 10 -> 10, of which waited for: 5 -> 4; matrix products, arithmetic and copies ran while one was open for 0% -> 0% of each run, Pallas kernels for 8% -> 9%
where the time goes in v3:
time: 95.1 us; the launch traced here: 94.6 us
  starting transfers between devices  35.4 us (37%)
  blocking collectives  31.5 us (33%)
  waiting for transfers between devices  13.9 us (15%)
  Pallas kernels  12.9 us (14%)
    all_to_all x1, blocking collectives, on_device(): lax.all_to_all(part, ('x', 'y'), 0, 0, axis_index_groups=[ORDER_XY], tile...  31.5 us
    all_to_all x1, starting transfers between devices, on_device(): lax.all_to_all(plane, 'zh', 0, 0, axis_index_groups=[ORDER_ZH], tiled=True)  16.1 us
    pallas_call x5, Pallas kernels, call(): pl.pallas_call(kernel, out_shape=outs, in_specs=specs, out_specs=tuple((p...  12.9 us
    ppermute x1, waiting for transfers between devices, on_device(): far = lax.ppermute(own, 'zl', [(0, 2), (2, 0), (1, 3), (3, 1)])  6.99 us
    ppermute x3, starting transfers between devices, swap_cores(): return lax.ppermute(piece, 'core', [(0, 1), (1, 0)])  5.75 us
    ppermute x1, starting transfers between devices, on_device(): far = lax.ppermute(own, 'zl', [(0, 2), (2, 0), (1, 3), (3, 1)])  5.18 us
    ppermute x1, waiting for transfers between devices, on_device(): outer = lax.ppermute(far, 'zl', [(1, 0), (2, 3)])  4.12 us
    ppermute x1, starting transfers between devices, on_device(): near = lax.ppermute(own, 'zl', [(0, 1), (1, 0), (2, 3), (3, 2)])  3.83 us
  transfers between devices with their start and end apart: 10, of which 4 were waited for; matrix products, arithmetic and copies ran while one was open for 0% of the time, Pallas kernels for 9%

profile of v3, /device:TPU:8, one launch (start us, length us, event | category | flops | bytes accessed | tf_op | source)
XLA Modules:
  0.0 94.6 jit_solution(6148314097701623290)
XLA Ops:
  0.6 5.2 %collective-permute-start.1 = (bf16[64,2560]{1,0:T(8,128)(2,1)}, bf16[64,2560]{1,0:T(8,128)(2,1)S(1)}, u32[]{:S(2)}, u32[]{:S(2)}) collective-permute-start(bf16[64,2560]{1,0:T(8,128)(2,1)} %refs_3_.2), channel_id=1, source_target_pairs={{0,4},{4,0},{2,6},{6,2},{1,5},{5,1},{3,7},{7,3},{8,12},{12,8},{10,... | collective-permute-start | bytes 983048 | tf_op jit(solution)/shard_map/ppermute | solution.py:169
  5.8 1.9 %collective-permute-start.2 = (bf16[64,2560]{1,0:T(8,128)(2,1)}, bf16[64,2560]{1,0:T(8,128)(2,1)S(1)}, u32[]{:S(2)}, u32[]{:S(2)}) collective-permute-start(bf16[64,2560]{1,0:T(8,128)(2,1)} %refs_3_.2), channel_id=1, source_target_pairs={{0,1},{1,0},{2,3},{3,2},{4,5},{5,4},{6,7},{7,6},{8,9},{9,8},{10,11... | collective-permute-start | bytes 983048 | tf_op jit(solution)/shard_map/ppermute | solution.py:152
  7.7 3.8 %collective-permute-start = (bf16[64,2560]{1,0:T(8,128)(2,1)}, bf16[64,2560]{1,0:T(8,128)(2,1)S(1)}, u32[]{:S(2)}, u32[]{:S(2)}) collective-permute-start(bf16[64,2560]{1,0:T(8,128)(2,1)} %refs_3_.2), channel_id=1, source_target_pairs={{0,2},{2,0},{4,6},{6,4},{1,3},{3,1},{5,7},{7,5},{8,10},{10,8},{12,... | collective-permute-start | bytes 983048 | tf_op jit(solution)/shard_map/ppermute | solution.py:171
  11.6 0.7 collective-permute-start.3
  12.3 2.4 %attended.1 = (bf16[512,384]{1,0:T(8,128)(2,1)S(1)}, bf16[64,2560]{1,0:T(8,128)(2,1)S(1)}) custom-call(bf16[512,384]{1,0:T(8,128)(2,1)} %refs_0_.3, bf16[512,384]{1,0:T(8,128)(2,1)} %refs_1_.3, bf16[512,384]{1,0:T(8,128)(2,1)} %refs_3_.3, bf16[64,2560]{1,0:T(8,128)(2,1)} %refs_3_.2), custom_call_target="tpu_custom_call" | custom-call | tf_op jit(solution)/shard_map/attended/pallas_call | solution.py:137
  14.6 7.0 %collective-permute-done.1.refs_2_ = bf16[64,2560]{1,0:T(8,128)(2,1)S(1)} collective-permute-done((bf16[64,2560]{1,0:T(8,128)(2,1)}, bf16[64,2560]{1,0:T(8,128)(2,1)S(1)}, u32[]{:S(2)}, u32[]{:S(2)}) %collective-permute-start.1) | collective-permute-done | bytes 327712 | tf_op jit(solution)/shard_map/ppermute | solution.py:169
  21.6 0.0 collective-permute-done.2.refs_5_
  21.6 1.3 %collective-permute-start.4 = (bf16[64,2560]{1,0:T(8,128)(2,1)S(1)}, bf16[64,2560]{1,0:T(8,128)(2,1)S(1)}, u32[]{:S(2)}, u32[]{:S(2)}) collective-permute-start(bf16[64,2560]{1,0:T(8,128)(2,1)S(1)} %collective-permute-done.1.refs_2_), channel_id=1, source_target_pairs={{2,0},{4,6},{3,1},{5,7},{10,8},{12,14},{11,9},{13,15},{18,16},{20,... | collective-permute-start | bytes 983048 | tf_op jit(solution)/shard_map/ppermute | solution.py:186
  22.9 1.9 %collective-permute-start.6 = (bf16[64,2560]{1,0:T(8,128)(2,1)S(1)}, bf16[64,2560]{1,0:T(8,128)(2,1)S(1)}, u32[]{:S(2)}, u32[]{:S(2)}) collective-permute-start(bf16[64,2560]{1,0:T(8,128)(2,1)S(1)} %collective-permute-done.1.refs_2_), channel_id=1, source_target_pairs={{0,1},{1,0},{2,3},{3,2},{4,5},{5,4},{6,7},{7,6},{8,9},{9,8},{10,11... | collective-permute-start | bytes 983048 | tf_op jit(solution)/shard_map/ppermute | solution.py:152
  24.8 1.2 %collective-permute-done.refs_1_ = bf16[64,2560]{1,0:T(8,128)(2,1)S(1)} collective-permute-done((bf16[64,2560]{1,0:T(8,128)(2,1)}, bf16[64,2560]{1,0:T(8,128)(2,1)S(1)}, u32[]{:S(2)}, u32[]{:S(2)}) %collective-permute-start) | collective-permute-done | bytes 327712 | tf_op jit(solution)/shard_map/ppermute | solution.py:171
  26.0 1.9 %collective-permute-start.5 = (bf16[64,2560]{1,0:T(8,128)(2,1)S(1)}, bf16[64,2560]{1,0:T(8,128)(2,1)S(1)}, u32[]{:S(2)}, u32[]{:S(2)}) collective-permute-start(bf16[64,2560]{1,0:T(8,128)(2,1)S(1)} %collective-permute-done.refs_1_), channel_id=1, source_target_pairs={{0,1},{1,0},{2,3},{3,2},{4,5},{5,4},{6,7},{7,6},{8,9},{9,8},{10,11... | collective-permute-start | bytes 983048 | tf_op jit(solution)/shard_map/ppermute | solution.py:152
  27.9 0.0 collective-permute-done.3.refs_3_
  27.9 0.7 collective-permute-start.7
  28.6 4.1 %collective-permute-done.4.refs_4_ = bf16[64,2560]{1,0:T(8,128)(2,1)S(1)} collective-permute-done((bf16[64,2560]{1,0:T(8,128)(2,1)S(1)}, bf16[64,2560]{1,0:T(8,128)(2,1)S(1)}, u32[]{:S(2)}, u32[]{:S(2)}) %collective-permute-start.4) | collective-permute-done | bytes 327712 | tf_op jit(solution)/shard_map/ppermute | solution.py:186
  32.7 1.9 %collective-permute-start.8 = (bf16[64,2560]{1,0:T(8,128)(2,1)S(1)}, bf16[64,2560]{1,0:T(8,128)(2,1)}, u32[]{:S(2)}, u32[]{:S(2)}) collective-permute-start(bf16[64,2560]{1,0:T(8,128)(2,1)S(1)} %collective-permute-done.4.refs_4_), channel_id=1, source_target_pairs={{0,1},{1,0},{6,7},{7,6},{8,9},{9,8},{14,15},{15,14},{16,17},{17,16... | collective-permute-start | bytes 983048 | tf_op jit(solution)/shard_map/ppermute | solution.py:154
  34.7 0.1 pad_add_fusion.place_ref
  34.7 0.0 collective-permute-done.5.refs_6_
  34.7 0.0 collective-permute-done.7.refs_8_
  34.7 0.0 collective-permute-done.6.refs_7_
  34.7 1.6 %collective-permute-done.8.refs_9_ = bf16[64,2560]{1,0:T(8,128)(2,1)} collective-permute-done((bf16[64,2560]{1,0:T(8,128)(2,1)S(1)}, bf16[64,2560]{1,0:T(8,128)(2,1)}, u32[]{:S(2)}, u32[]{:S(2)}) %collective-permute-start.8) | collective-permute-done | bytes 327712 | tf_op jit(solution)/shard_map/ppermute | solution.py:154
  36.4 2.7 %weight.1 = (bf16[16,4,40,384]{3,2,1,0:T(8,128)(2,1)S(1)}, bf16[4,2,64,2560]{3,2,1,0:T(8,128)(2,1)}) custom-call(s32[2]{0:T(128)S(1)} %pad_add_fusion.place_ref, bf16[64,2560]{1,0:T(8,128)(2,1)S(1)} %get-tuple-element.16.refs_0_, bf16[64,2560]{1,0:T(8,128)(2,1)S(1)} %collective-permute-done.refs_1_, bf16[64,2560]{1,0:T(8,128)(2,1)S(1)} %collective-permute-done.1.refs_2_, ...), custom_call_target="tpu_custom_call" | custom-call | tf_op jit(solution)/shard_map/weight/pallas_call | solution.py:137
  39.1 0.0 copy-start
  39.1 31.5 %all_to_all.10.got_ref = bf16[16,4,40,384]{3,2,1,0:T(8,128)(2,1)S(1)} all-to-all(bf16[16,4,40,384]{3,2,1,0:T(8,128)(2,1)S(1)} %get-tuple-element.22), channel_id=1, replica_groups={{80,88,64,72,112,120,96,104,16,24,0,8,48,56,32,40},{81,89,65,73,113,121..., dimensions={0} | all-to-all | bytes 3932160 | tf_op jit(solution)/shard_map/all_to_all | solution.py:215
  70.7 0.9 sum.1
  71.6 16.1 %all-to-all-start.1 = ((bf16[4,40,384]{2,1,0:T(8,128)(2,1)}), bf16[4,40,384]{2,1,0:T(8,128)(2,1)S(1)}, u32[]{:S(2)}, u32[]{:S(2)}) async-start(bf16[4,40,384]{2,1,0:T(8,128)(2,1)} %sum.1), calls=%async_computation.1 | async-start | bytes 245760 | tf_op jit(solution)/shard_map/all_to_all | solution.py:218
  87.7 0.0 copy-done
  87.7 6.3 %backward.1 = (bf16[512,384]{1,0:T(8,128)(2,1)}, bf16[512,384]{1,0:T(8,128)(2,1)}, bf16[512,384]{1,0:T(8,128)(2,1)}) custom-call(bf16[512,2560]{1,0:T(8,128)(2,1)S(1)} %bitcast.3, bf16[512,384]{1,0:T(8,128)(2,1)} %refs_0_.3, bf16[512,384]{1,0:T(8,128)(2,1)} %refs_1_.3, bf16[2560,384]{1,0:T(8,128)(2,1)} %refs_2_.3, bf16[512,384]{1,0:T(8,128)(2,1)} %refs_3_.3), custom_call_target="tpu_custom_call" | custom-call | tf_op jit(solution)/shard_map/backward/pallas_call | solution.py:137
  93.9 0.0 all-to-all-done.1.a
  93.9 0.6 mean.1
Async XLA Ops:
  0.6 21.0 %collective-permute-start.1 = (bf16[64,2560]{1,0:T(8,128)(2,1)}, bf16[64,2560]{1,0:T(8,128)(2,1)S(1)}, u32[]{:S(2)}, u32[]{:S(2)}) collective-permute-start(bf16[64,2560]{1,0:T(8,128)(2,1)} %refs_3_.2), channel_id=1, source_target_pairs={{0,4},{4,0},{2,6},{6,2},{1,5},{5,1},{3,7},{7,3},{8,12},{12,8},{10,... | collective-permute-start | bytes 983048 | tf_op jit(solution)/shard_map/ppermute | solution.py:169
  5.8 15.8 %collective-permute-start.2 = (bf16[64,2560]{1,0:T(8,128)(2,1)}, bf16[64,2560]{1,0:T(8,128)(2,1)S(1)}, u32[]{:S(2)}, u32[]{:S(2)}) collective-permute-start(bf16[64,2560]{1,0:T(8,128)(2,1)} %refs_3_.2), channel_id=1, source_target_pairs={{0,1},{1,0},{2,3},{3,2},{4,5},{5,4},{6,7},{7,6},{8,9},{9,8},{10,11... | collective-permute-start | bytes 983048 | tf_op jit(solution)/shard_map/ppermute | solution.py:152
  7.7 18.3 %collective-permute-start = (bf16[64,2560]{1,0:T(8,128)(2,1)}, bf16[64,2560]{1,0:T(8,128)(2,1)S(1)}, u32[]{:S(2)}, u32[]{:S(2)}) collective-permute-start(bf16[64,2560]{1,0:T(8,128)(2,1)} %refs_3_.2), channel_id=1, source_target_pairs={{0,2},{2,0},{4,6},{6,4},{1,3},{3,1},{5,7},{7,5},{8,10},{10,8},{12,... | collective-permute-start | bytes 983048 | tf_op jit(solution)/shard_map/ppermute | solution.py:171
  11.6 16.3 %collective-permute-start.3 = (bf16[64,2560]{1,0:T(8,128)(2,1)}, bf16[64,2560]{1,0:T(8,128)(2,1)S(1)}, u32[]{:S(2)}, u32[]{:S(2)}) collective-permute-start(bf16[64,2560]{1,0:T(8,128)(2,1)} %refs_3_.2), channel_id=1, source_target_pairs={{2,4},{4,2},{3,5},{5,3},{10,12},{12,10},{11,13},{13,11},{18,20},{2... | collective-permute-start | bytes 983048 | tf_op jit(solution)/shard_map/ppermute | solution.py:170
  21.6 11.1 %collective-permute-start.4 = (bf16[64,2560]{1,0:T(8,128)(2,1)S(1)}, bf16[64,2560]{1,0:T(8,128)(2,1)S(1)}, u32[]{:S(2)}, u32[]{:S(2)}) collective-permute-start(bf16[64,2560]{1,0:T(8,128)(2,1)S(1)} %collective-permute-done.1.refs_2_), channel_id=1, source_target_pairs={{2,0},{4,6},{3,1},{5,7},{10,8},{12,14},{11,9},{13,15},{18,16},{20,... | collective-permute-start | bytes 983048 | tf_op jit(solution)/shard_map/ppermute | solution.py:186
  22.9 11.8 %collective-permute-start.6 = (bf16[64,2560]{1,0:T(8,128)(2,1)S(1)}, bf16[64,2560]{1,0:T(8,128)(2,1)S(1)}, u32[]{:S(2)}, u32[]{:S(2)}) collective-permute-start(bf16[64,2560]{1,0:T(8,128)(2,1)S(1)} %collective-permute-done.1.refs_2_), channel_id=1, source_target_pairs={{0,1},{1,0},{2,3},{3,2},{4,5},{5,4},{6,7},{7,6},{8,9},{9,8},{10,11... | collective-permute-start | bytes 983048 | tf_op jit(solution)/shard_map/ppermute | solution.py:152
  26.0 8.7 %collective-permute-start.5 = (bf16[64,2560]{1,0:T(8,128)(2,1)S(1)}, bf16[64,2560]{1,0:T(8,128)(2,1)S(1)}, u32[]{:S(2)}, u32[]{:S(2)}) collective-permute-start(bf16[64,2560]{1,0:T(8,128)(2,1)S(1)} %collective-permute-done.refs_1_), channel_id=1, source_target_pairs={{0,1},{1,0},{2,3},{3,2},{4,5},{5,4},{6,7},{7,6},{8,9},{9,8},{10,11... | collective-permute-start | bytes 983048 | tf_op jit(solution)/shard_map/ppermute | solution.py:152
  27.9 6.8 %collective-permute-start.7 = (bf16[64,2560]{1,0:T(8,128)(2,1)S(1)}, bf16[64,2560]{1,0:T(8,128)(2,1)S(1)}, u32[]{:S(2)}, u32[]{:S(2)}) collective-permute-start(bf16[64,2560]{1,0:T(8,128)(2,1)S(1)} %collective-permute-done.3.refs_3_), channel_id=1, source_target_pairs={{2,3},{3,2},{4,5},{5,4},{10,11},{11,10},{12,13},{13,12},{18,19},{1... | collective-permute-start | bytes 983048 | tf_op jit(solution)/shard_map/ppermute | solution.py:154
  32.7 3.6 %collective-permute-start.8 = (bf16[64,2560]{1,0:T(8,128)(2,1)S(1)}, bf16[64,2560]{1,0:T(8,128)(2,1)}, u32[]{:S(2)}, u32[]{:S(2)}) collective-permute-start(bf16[64,2560]{1,0:T(8,128)(2,1)S(1)} %collective-permute-done.4.refs_4_), channel_id=1, source_target_pairs={{0,1},{1,0},{6,7},{7,6},{8,9},{9,8},{14,15},{15,14},{16,17},{17,16... | collective-permute-start | bytes 983048 | tf_op jit(solution)/shard_map/ppermute | solution.py:154
  39.1 48.5 %copy-start = (bf16[4,2,64,2560]{3,2,1,0:T(8,128)(2,1)S(1)}, bf16[4,2,64,2560]{3,2,1,0:T(8,128)(2,1)}, u32[]{:S(2)}) copy-start(bf16[4,2,64,2560]{3,2,1,0:T(8,128)(2,1)} %get-tuple-element.23) | copy-start | bytes 7864324
  71.6 22.3 %all-to-all-start.1 = ((bf16[4,40,384]{2,1,0:T(8,128)(2,1)}), bf16[4,40,384]{2,1,0:T(8,128)(2,1)S(1)}, u32[]{:S(2)}, u32[]{:S(2)}) async-start(bf16[4,40,384]{2,1,0:T(8,128)(2,1)} %sum.1), calls=%async_computation.1 | async-start | bytes 245760 | tf_op jit(solution)/shard_map/all_to_all | solution.py:218

commit v4 on v3

--- a/solution.py
+++ b/solution.py
@@ -102,21 +102,20 @@
     out_ref[...] = total * scale
 
 
-def backward_kernel(rows_ref, *refs):
-    ins, (gq_ref, gk_ref, gv_ref) = refs[:4], refs[4:7]
-    q_ref, k_ref, w_ref, v_ref, first_ref, second_ref, g_ref, sems = refs[7:]
-    copies = fetch(ins, (q_ref, k_ref, w_ref, v_ref), sems)
-    copies[0].wait()
-    copies[1].wait()
+def backward_kernel(rows_ref, q_ref, k_ref, *refs):
+    ins, (gq_ref, gk_ref, gv_ref) = refs[:2], refs[2:5]
+    w_ref, v_ref, first_ref, second_ref, g_ref, sems = refs[5:]
+    copies = fetch(ins, (w_ref, v_ref), sems)
     for i, at in enumerate(tiles(gq_ref.shape)):
         q, k = q_ref[at], k_ref[at]
         for ref, half in zip((first_ref, second_ref), HALVES):
             ref[i] = half_probs(q, k, *half)
-    copies[2].wait()
+    copies[0].wait()
     g_ref[...] = dot(rows_ref[...], w_ref[...], 1, 0).astype(BF16)
-    copies[3].wait()
+    copies[1].wait()
+    saved = []
     for i, at in enumerate(tiles(gq_ref.shape)):
-        q, k, v, g = q_ref[at], k_ref[at], v_ref[at], g_ref[at]
+        v, g = v_ref[at], g_ref[at]
         probs_low, grad_scores = [], []
         for ref, (start, end) in zip((first_ref, second_ref), HALVES):
             probs = ref[i]
@@ -124,10 +123,11 @@
             row_total = jnp.sum(probs * grad_probs, axis=1, keepdims=True)
             probs_low.append(probs.astype(BF16))
             grad_scores.append((probs * (grad_probs - row_total) * SCALING).astype(BF16))
-        probs_low, grad_scores = widened(*probs_low), widened(*grad_scores)
-        gv_ref[at] = dot(probs_low, g, 0, 0).astype(BF16)
-        gq_ref[at] = dot(grad_scores, k, 1, 0).astype(BF16)
-        gk_ref[at] = dot(grad_scores, q, 0, 0).astype(BF16)
+        saved.append((widened(*probs_low), widened(*grad_scores)))
+    for (probs_low, grad_scores), at in zip(saved, tiles(gq_ref.shape)):
+        gv_ref[at] = dot(probs_low, g_ref[at], 0, 0).astype(BF16)
+        gq_ref[at] = dot(grad_scores, k_ref[at], 1, 0).astype(BF16)
+        gk_ref[at] = dot(grad_scores, q_ref[at], 0, 0).astype(BF16)
 
 
 def call(kernel, name, outs, *args, mib=48, spaces=(), out_spaces=None, scratch=()):
@@ -221,19 +221,16 @@
         "backward",
         (same, same, same),
         rows.reshape(shape[0], d),
-        *(
-            pltpu.with_memory_space_constraint(a, pltpu.HBM)
-            for a in (queries, key_rows, out_weight, value_rows)
-        ),
-        spaces=[pltpu.VMEM] + [pltpu.HBM] * 4,
+        queries,
+        key_rows,
+        *(pltpu.with_memory_space_constraint(a, pltpu.HBM) for a in (out_weight, value_rows)),
+        spaces=[pltpu.VMEM] * 3 + [pltpu.HBM] * 2,
         scratch=[
-            pltpu.VMEM(shape, BF16),
-            pltpu.VMEM(shape, BF16),
             pltpu.VMEM(out_weight.shape, BF16),
             pltpu.VMEM(shape, BF16),
             *(pltpu.VMEM((n_tiles, end - at, end), F32) for at, end in HALVES),
             pltpu.VMEM(shape, BF16),
-            pltpu.SemaphoreType.DMA((4,)),
+            pltpu.SemaphoreType.DMA((2,)),
         ],
     )
     grad_weight = call(

time: 95.1 us -> 94.2 us (level)
  Pallas kernels: 12.9 us -> 11.3 us
    pallas_call x5, Pallas kernels: 12.9 us -> 11.3 us  [call(): pl.pallas_call(kernel, out_shape=outs, in_specs=specs, out_specs=tuple((p...]
  transfers between devices with their start and end apart: 10 -> 10, of which waited for: 4 -> 4; matrix products, arithmetic and copies ran while one was open for 0% -> 0% of each run, Pallas kernels for 9% -> 8%
where the time goes in v4:
time: 94.2 us; the launch traced here: 93.7 us
  starting transfers between devices  35.4 us (38%)
  blocking collectives  31.5 us (33%)
  waiting for transfers between devices  13.9 us (15%)
  Pallas kernels  11.3 us (12%)
    all_to_all x1, blocking collectives, on_device(): lax.all_to_all(part, ('x', 'y'), 0, 0, axis_index_groups=[ORDER_XY], tile...  31.5 us
    all_to_all x1, starting transfers between devices, on_device(): lax.all_to_all(plane, 'zh', 0, 0, axis_index_groups=[ORDER_ZH], tiled=True)  16.1 us
    pallas_call x5, Pallas kernels, call(): pl.pallas_call(kernel, out_shape=outs, in_specs=specs, out_specs=tuple((p...  11.3 us
    ppermute x1, waiting for transfers between devices, on_device(): far = lax.ppermute(own, 'zl', [(0, 2), (2, 0), (1, 3), (3, 1)])  6.99 us
    ppermute x3, starting transfers between devices, swap_cores(): return lax.ppermute(piece, 'core', [(0, 1), (1, 0)])  5.75 us
    ppermute x1, starting transfers between devices, on_device(): far = lax.ppermute(own, 'zl', [(0, 2), (2, 0), (1, 3), (3, 1)])  5.18 us
    ppermute x1, waiting for transfers between devices, on_device(): outer = lax.ppermute(far, 'zl', [(1, 0), (2, 3)])  4.12 us
    ppermute x1, starting transfers between devices, on_device(): near = lax.ppermute(own, 'zl', [(0, 1), (1, 0), (2, 3), (3, 2)])  3.83 us
  transfers between devices with their start and end apart: 10, of which 4 were waited for; matrix products, arithmetic and copies ran while one was open for 0% of the time, Pallas kernels for 8%

profile of v4, /device:TPU:8, one launch (start us, length us, event | category | flops | bytes accessed | tf_op | source)
XLA Modules:
  0.0 93.7 jit_solution(10889968064435593295)
XLA Ops:
  0.6 5.2 %collective-permute-start.1 = (bf16[64,2560]{1,0:T(8,128)(2,1)}, bf16[64,2560]{1,0:T(8,128)(2,1)S(1)}, u32[]{:S(2)}, u32[]{:S(2)}) collective-permute-start(bf16[64,2560]{1,0:T(8,128)(2,1)} %refs_3_.1), channel_id=1, source_target_pairs={{0,4},{4,0},{2,6},{6,2},{1,5},{5,1},{3,7},{7,3},{8,12},{12,8},{10,... | collective-permute-start | bytes 983048 | tf_op jit(solution)/shard_map/ppermute | solution.py:169
  5.8 1.9 %collective-permute-start.2 = (bf16[64,2560]{1,0:T(8,128)(2,1)}, bf16[64,2560]{1,0:T(8,128)(2,1)S(1)}, u32[]{:S(2)}, u32[]{:S(2)}) collective-permute-start(bf16[64,2560]{1,0:T(8,128)(2,1)} %refs_3_.1), channel_id=1, source_target_pairs={{0,1},{1,0},{2,3},{3,2},{4,5},{5,4},{6,7},{7,6},{8,9},{9,8},{10,11... | collective-permute-start | bytes 983048 | tf_op jit(solution)/shard_map/ppermute | solution.py:152
  7.7 3.8 %collective-permute-start = (bf16[64,2560]{1,0:T(8,128)(2,1)}, bf16[64,2560]{1,0:T(8,128)(2,1)S(1)}, u32[]{:S(2)}, u32[]{:S(2)}) collective-permute-start(bf16[64,2560]{1,0:T(8,128)(2,1)} %refs_3_.1), channel_id=1, source_target_pairs={{0,2},{2,0},{4,6},{6,4},{1,3},{3,1},{5,7},{7,5},{8,10},{10,8},{12,... | collective-permute-start | bytes 983048 | tf_op jit(solution)/shard_map/ppermute | solution.py:171
  11.6 0.7 collective-permute-start.3
  12.3 2.4 %attended.1 = (bf16[512,384]{1,0:T(8,128)(2,1)S(1)}, bf16[64,2560]{1,0:T(8,128)(2,1)S(1)}) custom-call(bf16[512,384]{1,0:T(8,128)(2,1)} %q_ref.1, bf16[512,384]{1,0:T(8,128)(2,1)} %k_ref.1, bf16[512,384]{1,0:T(8,128)(2,1)} %refs_1_.3, bf16[64,2560]{1,0:T(8,128)(2,1)} %refs_3_.1), custom_call_target="tpu_custom_call" | custom-call | tf_op jit(solution)/shard_map/attended/pallas_call | solution.py:137
  14.6 7.0 %collective-permute-done.1.refs_2_ = bf16[64,2560]{1,0:T(8,128)(2,1)S(1)} collective-permute-done((bf16[64,2560]{1,0:T(8,128)(2,1)}, bf16[64,2560]{1,0:T(8,128)(2,1)S(1)}, u32[]{:S(2)}, u32[]{:S(2)}) %collective-permute-start.1) | collective-permute-done | bytes 327712 | tf_op jit(solution)/shard_map/ppermute | solution.py:169
  21.6 0.0 collective-permute-done.2.refs_5_
  21.6 1.3 %collective-permute-start.4 = (bf16[64,2560]{1,0:T(8,128)(2,1)S(1)}, bf16[64,2560]{1,0:T(8,128)(2,1)S(1)}, u32[]{:S(2)}, u32[]{:S(2)}) collective-permute-start(bf16[64,2560]{1,0:T(8,128)(2,1)S(1)} %collective-permute-done.1.refs_2_), channel_id=1, source_target_pairs={{2,0},{4,6},{3,1},{5,7},{10,8},{12,14},{11,9},{13,15},{18,16},{20,... | collective-permute-start | bytes 983048 | tf_op jit(solution)/shard_map/ppermute | solution.py:186
  22.9 1.9 %collective-permute-start.6 = (bf16[64,2560]{1,0:T(8,128)(2,1)S(1)}, bf16[64,2560]{1,0:T(8,128)(2,1)S(1)}, u32[]{:S(2)}, u32[]{:S(2)}) collective-permute-start(bf16[64,2560]{1,0:T(8,128)(2,1)S(1)} %collective-permute-done.1.refs_2_), channel_id=1, source_target_pairs={{0,1},{1,0},{2,3},{3,2},{4,5},{5,4},{6,7},{7,6},{8,9},{9,8},{10,11... | collective-permute-start | bytes 983048 | tf_op jit(solution)/shard_map/ppermute | solution.py:152
  24.8 1.2 %collective-permute-done.refs_1_ = bf16[64,2560]{1,0:T(8,128)(2,1)S(1)} collective-permute-done((bf16[64,2560]{1,0:T(8,128)(2,1)}, bf16[64,2560]{1,0:T(8,128)(2,1)S(1)}, u32[]{:S(2)}, u32[]{:S(2)}) %collective-permute-start) | collective-permute-done | bytes 327712 | tf_op jit(solution)/shard_map/ppermute | solution.py:171
  26.0 1.9 %collective-permute-start.5 = (bf16[64,2560]{1,0:T(8,128)(2,1)S(1)}, bf16[64,2560]{1,0:T(8,128)(2,1)S(1)}, u32[]{:S(2)}, u32[]{:S(2)}) collective-permute-start(bf16[64,2560]{1,0:T(8,128)(2,1)S(1)} %collective-permute-done.refs_1_), channel_id=1, source_target_pairs={{0,1},{1,0},{2,3},{3,2},{4,5},{5,4},{6,7},{7,6},{8,9},{9,8},{10,11... | collective-permute-start | bytes 983048 | tf_op jit(solution)/shard_map/ppermute | solution.py:152
  27.9 0.0 collective-permute-done.3.refs_3_
  27.9 0.7 collective-permute-start.7
  28.6 4.1 %collective-permute-done.4.refs_4_ = bf16[64,2560]{1,0:T(8,128)(2,1)S(1)} collective-permute-done((bf16[64,2560]{1,0:T(8,128)(2,1)S(1)}, bf16[64,2560]{1,0:T(8,128)(2,1)S(1)}, u32[]{:S(2)}, u32[]{:S(2)}) %collective-permute-start.4) | collective-permute-done | bytes 327712 | tf_op jit(solution)/shard_map/ppermute | solution.py:186
  32.7 1.9 %collective-permute-start.8 = (bf16[64,2560]{1,0:T(8,128)(2,1)S(1)}, bf16[64,2560]{1,0:T(8,128)(2,1)}, u32[]{:S(2)}, u32[]{:S(2)}) collective-permute-start(bf16[64,2560]{1,0:T(8,128)(2,1)S(1)} %collective-permute-done.4.refs_4_), channel_id=1, source_target_pairs={{0,1},{1,0},{6,7},{7,6},{8,9},{9,8},{14,15},{15,14},{16,17},{17,16... | collective-permute-start | bytes 983048 | tf_op jit(solution)/shard_map/ppermute | solution.py:154
  34.7 0.1 pad_add_fusion.place_ref
  34.7 0.0 collective-permute-done.5.refs_6_
  34.7 0.0 collective-permute-done.7.refs_8_
  34.7 0.0 collective-permute-done.6.refs_7_
  34.7 1.6 %collective-permute-done.8.refs_9_ = bf16[64,2560]{1,0:T(8,128)(2,1)} collective-permute-done((bf16[64,2560]{1,0:T(8,128)(2,1)S(1)}, bf16[64,2560]{1,0:T(8,128)(2,1)}, u32[]{:S(2)}, u32[]{:S(2)}) %collective-permute-start.8) | collective-permute-done | bytes 327712 | tf_op jit(solution)/shard_map/ppermute | solution.py:154
  36.4 2.7 %weight.1 = (bf16[16,4,40,384]{3,2,1,0:T(8,128)(2,1)S(1)}, bf16[4,2,64,2560]{3,2,1,0:T(8,128)(2,1)}) custom-call(s32[2]{0:T(128)S(1)} %pad_add_fusion.place_ref, bf16[64,2560]{1,0:T(8,128)(2,1)S(1)} %get-tuple-element.16.refs_0_, bf16[64,2560]{1,0:T(8,128)(2,1)S(1)} %collective-permute-done.refs_1_, bf16[64,2560]{1,0:T(8,128)(2,1)S(1)} %collective-permute-done.1.refs_2_, ...), custom_call_target="tpu_custom_call" | custom-call | tf_op jit(solution)/shard_map/weight/pallas_call | solution.py:137
  39.1 0.0 copy-start
  39.1 31.5 %all_to_all.10.got_ref = bf16[16,4,40,384]{3,2,1,0:T(8,128)(2,1)S(1)} all-to-all(bf16[16,4,40,384]{3,2,1,0:T(8,128)(2,1)S(1)} %get-tuple-element.22), channel_id=1, replica_groups={{80,88,64,72,112,120,96,104,16,24,0,8,48,56,32,40},{81,89,65,73,113,121..., dimensions={0} | all-to-all | bytes 3932160 | tf_op jit(solution)/shard_map/all_to_all | solution.py:215
  70.7 0.0 copy-start.1
  70.7 0.0 copy-start.2
  70.7 0.3 sum.1
  70.9 0.0 copy-start.3
  71.0 0.6 copy-done.3
  71.6 16.1 %all-to-all-start.1 = ((bf16[4,40,384]{2,1,0:T(8,128)(2,1)}), bf16[4,40,384]{2,1,0:T(8,128)(2,1)S(1)}, u32[]{:S(2)}, u32[]{:S(2)}) async-start(bf16[4,40,384]{2,1,0:T(8,128)(2,1)} %copy-done.3), calls=%async_computation.1 | async-start | bytes 245760 | tf_op jit(solution)/shard_map/all_to_all | solution.py:218
  87.7 0.0 copy-done
  87.7 0.0 copy-done.1
  87.7 0.0 copy-done.2
  87.7 5.3 %backward.1 = (bf16[512,384]{1,0:T(8,128)(2,1)}, bf16[512,384]{1,0:T(8,128)(2,1)}, bf16[512,384]{1,0:T(8,128)(2,1)}) custom-call(bf16[512,2560]{1,0:T(8,128)(2,1)S(1)} %bitcast.3, bf16[512,384]{1,0:T(8,128)(2,1)S(1)} %copy-done.1, bf16[512,384]{1,0:T(8,128)(2,1)S(1)} %copy-done.2, bf16[2560,384]{1,0:T(8,128)(2,1)} %refs_0_.3, bf16[512,384]{1,0:T(8,128)(2,1)} %refs_1_.3), custom_call_target="tpu_custom_call" | custom-call | tf_op jit(solution)/shard_map/backward/pallas_call | solution.py:137
  93.0 0.0 all-to-all-done.1.a
  93.0 0.6 mean.1
Async XLA Ops:
  0.6 21.0 %collective-permute-start.1 = (bf16[64,2560]{1,0:T(8,128)(2,1)}, bf16[64,2560]{1,0:T(8,128)(2,1)S(1)}, u32[]{:S(2)}, u32[]{:S(2)}) collective-permute-start(bf16[64,2560]{1,0:T(8,128)(2,1)} %refs_3_.1), channel_id=1, source_target_pairs={{0,4},{4,0},{2,6},{6,2},{1,5},{5,1},{3,7},{7,3},{8,12},{12,8},{10,... | collective-permute-start | bytes 983048 | tf_op jit(solution)/shard_map/ppermute | solution.py:169
  5.8 15.8 %collective-permute-start.2 = (bf16[64,2560]{1,0:T(8,128)(2,1)}, bf16[64,2560]{1,0:T(8,128)(2,1)S(1)}, u32[]{:S(2)}, u32[]{:S(2)}) collective-permute-start(bf16[64,2560]{1,0:T(8,128)(2,1)} %refs_3_.1), channel_id=1, source_target_pairs={{0,1},{1,0},{2,3},{3,2},{4,5},{5,4},{6,7},{7,6},{8,9},{9,8},{10,11... | collective-permute-start | bytes 983048 | tf_op jit(solution)/shard_map/ppermute | solution.py:152
  7.7 18.3 %collective-permute-start = (bf16[64,2560]{1,0:T(8,128)(2,1)}, bf16[64,2560]{1,0:T(8,128)(2,1)S(1)}, u32[]{:S(2)}, u32[]{:S(2)}) collective-permute-start(bf16[64,2560]{1,0:T(8,128)(2,1)} %refs_3_.1), channel_id=1, source_target_pairs={{0,2},{2,0},{4,6},{6,4},{1,3},{3,1},{5,7},{7,5},{8,10},{10,8},{12,... | collective-permute-start | bytes 983048 | tf_op jit(solution)/shard_map/ppermute | solution.py:171
  11.6 16.3 %collective-permute-start.3 = (bf16[64,2560]{1,0:T(8,128)(2,1)}, bf16[64,2560]{1,0:T(8,128)(2,1)S(1)}, u32[]{:S(2)}, u32[]{:S(2)}) collective-permute-start(bf16[64,2560]{1,0:T(8,128)(2,1)} %refs_3_.1), channel_id=1, source_target_pairs={{2,4},{4,2},{3,5},{5,3},{10,12},{12,10},{11,13},{13,11},{18,20},{2... | collective-permute-start | bytes 983048 | tf_op jit(solution)/shard_map/ppermute | solution.py:170
  21.6 11.1 %collective-permute-start.4 = (bf16[64,2560]{1,0:T(8,128)(2,1)S(1)}, bf16[64,2560]{1,0:T(8,128)(2,1)S(1)}, u32[]{:S(2)}, u32[]{:S(2)}) collective-permute-start(bf16[64,2560]{1,0:T(8,128)(2,1)S(1)} %collective-permute-done.1.refs_2_), channel_id=1, source_target_pairs={{2,0},{4,6},{3,1},{5,7},{10,8},{12,14},{11,9},{13,15},{18,16},{20,... | collective-permute-start | bytes 983048 | tf_op jit(solution)/shard_map/ppermute | solution.py:186
  22.9 11.8 %collective-permute-start.6 = (bf16[64,2560]{1,0:T(8,128)(2,1)S(1)}, bf16[64,2560]{1,0:T(8,128)(2,1)S(1)}, u32[]{:S(2)}, u32[]{:S(2)}) collective-permute-start(bf16[64,2560]{1,0:T(8,128)(2,1)S(1)} %collective-permute-done.1.refs_2_), channel_id=1, source_target_pairs={{0,1},{1,0},{2,3},{3,2},{4,5},{5,4},{6,7},{7,6},{8,9},{9,8},{10,11... | collective-permute-start | bytes 983048 | tf_op jit(solution)/shard_map/ppermute | solution.py:152
  26.0 8.7 %collective-permute-start.5 = (bf16[64,2560]{1,0:T(8,128)(2,1)S(1)}, bf16[64,2560]{1,0:T(8,128)(2,1)S(1)}, u32[]{:S(2)}, u32[]{:S(2)}) collective-permute-start(bf16[64,2560]{1,0:T(8,128)(2,1)S(1)} %collective-permute-done.refs_1_), channel_id=1, source_target_pairs={{0,1},{1,0},{2,3},{3,2},{4,5},{5,4},{6,7},{7,6},{8,9},{9,8},{10,11... | collective-permute-start | bytes 983048 | tf_op jit(solution)/shard_map/ppermute | solution.py:152
  27.9 6.8 %collective-permute-start.7 = (bf16[64,2560]{1,0:T(8,128)(2,1)S(1)}, bf16[64,2560]{1,0:T(8,128)(2,1)S(1)}, u32[]{:S(2)}, u32[]{:S(2)}) collective-permute-start(bf16[64,2560]{1,0:T(8,128)(2,1)S(1)} %collective-permute-done.3.refs_3_), channel_id=1, source_target_pairs={{2,3},{3,2},{4,5},{5,4},{10,11},{11,10},{12,13},{13,12},{18,19},{1... | collective-permute-start | bytes 983048 | tf_op jit(solution)/shard_map/ppermute | solution.py:154
  32.7 3.6 %collective-permute-start.8 = (bf16[64,2560]{1,0:T(8,128)(2,1)S(1)}, bf16[64,2560]{1,0:T(8,128)(2,1)}, u32[]{:S(2)}, u32[]{:S(2)}) collective-permute-start(bf16[64,2560]{1,0:T(8,128)(2,1)S(1)} %collective-permute-done.4.refs_4_), channel_id=1, source_target_pairs={{0,1},{1,0},{6,7},{7,6},{8,9},{9,8},{14,15},{15,14},{16,17},{17,16... | collective-permute-start | bytes 983048 | tf_op jit(solution)/shard_map/ppermute | solution.py:154
  39.1 48.5 %copy-start = (bf16[4,2,64,2560]{3,2,1,0:T(8,128)(2,1)S(1)}, bf16[4,2,64,2560]{3,2,1,0:T(8,128)(2,1)}, u32[]{:S(2)}) copy-start(bf16[4,2,64,2560]{3,2,1,0:T(8,128)(2,1)} %get-tuple-element.23) | copy-start | bytes 7864324
  70.7 17.0 %copy-start.1 = (bf16[512,384]{1,0:T(8,128)(2,1)S(1)}, bf16[512,384]{1,0:T(8,128)(2,1)}, u32[]{:S(2)}) copy-start(bf16[512,384]{1,0:T(8,128)(2,1)} %q_ref.1) | copy-start | bytes 1179652
  70.7 17.0 %copy-start.2 = (bf16[512,384]{1,0:T(8,128)(2,1)S(1)}, bf16[512,384]{1,0:T(8,128)(2,1)}, u32[]{:S(2)}) copy-start(bf16[512,384]{1,0:T(8,128)(2,1)} %k_ref.1) | copy-start | bytes 1179652
  70.9 0.7 copy-start.3
  71.6 21.4 %all-to-all-start.1 = ((bf16[4,40,384]{2,1,0:T(8,128)(2,1)}), bf16[4,40,384]{2,1,0:T(8,128)(2,1)S(1)}, u32[]{:S(2)}, u32[]{:S(2)}) async-start(bf16[4,40,384]{2,1,0:T(8,128)(2,1)} %copy-done.3), calls=%async_computation.1 | async-start | bytes 245760 | tf_op jit(solution)/shard_map/all_to_all | solution.py:218
